TPU v7x, 256 devices: a whole 4x4x8 slice. The times are simulated.
256 devices in a mesh: grp: 8 (over y, x_lo), dev: 32 (over z, x_hi, core).
Axes of the slice: x: 4 (x_hi: 2, x_lo: 2; x = x_hi * 2 + x_lo), y: 4, z: 8, core: 2. Of those that a mesh axis runs over, the one named last changes fastest.
Arguments:
- border: bfloat16 [8, 131072, 1024], P('grp', 'dev'), may hold values from -1.5 to 1.5
- inverse_blocks: bfloat16 [8, 1024, 1024], P('grp')
- selected: int32 [256], replicated, may hold values from 0 to 131071, as said below
- assignment: int32 [8], replicated, may hold values from 0 to 7, each once
- probability: float32 [8], replicated, may hold values from 2 to 8
- prior_panel: bfloat16 [131072, 256], P(('dev', 'grp'))
Outputs:
- panel_out: float32 [131072, 256], P(('dev', 'grp'))
- residual: float32 [8, 1024, 256], P('grp', 'dev')
Inputs may be any that keep to these rules, and one draw needn't show every extreme that they name: `selected`: 256 distinct rows.
All inputs are finite; a program needn't handle non-finite values.
Results may differ from a plain program's by a relative error of at most 0.0005.
The roundings to bfloat16 on the way count: a program that leaves them out, or rounds other values in their place, can miss the bound.
Values may be sent and summed in bfloat16 or wider, within the bound.
A program may use at most 64 MiB of HBM per device.

v0:
```python
import math

import jax
import jax.numpy as jnp
from jax import lax
from jax.sharding import PartitionSpec as P

N1 = 131072


def take_rows(source, selected, first_row, count):
    offsets = selected - first_row
    inside = (offsets >= 0) & (offsets < count)
    picked = jnp.take(source, jnp.clip(offsets, 0, count - 1), axis=0).astype(jnp.float32)
    return jnp.where(inside[:, None], picked, 0.0)


def mark_rows(values, selected, first_row):
    row_ids = first_row + jnp.arange(values.shape[0], dtype=jnp.int32)
    marked = jnp.any(row_ids[:, None] == selected[None, :], axis=1)
    return jnp.where(marked[:, None], 0.0, values)


def body(border, inverse_blocks, selected, assignment, probability, prior_panel):
    groups = lax.axis_size("grp")
    group_index = lax.axis_index("grp")
    member = lax.axis_index("dev")
    my_rows = border[0]
    height = my_rows.shape[0]
    own_rows = prior_panel.shape[0]
    rank_list = jnp.arange(groups, dtype=jnp.int32)
    scenario = jnp.sum(jnp.where(rank_list == group_index, assignment, 0))
    weight = jnp.sum(jnp.where(rank_list == scenario, probability, 0.0))
    picked = take_rows(my_rows, selected, member * height, height)
    chosen = lax.psum(picked.astype(jnp.bfloat16), "dev")
    project = lax.dot_general(
        inverse_blocks[0], chosen, (((1,), (1,)), ((), ())), preferred_element_type=jnp.float32
    ).astype(jnp.bfloat16)
    first_row = (member * groups + group_index) * own_rows
    prior_pick = take_rows(prior_panel, selected, first_row, own_rows)
    prior_sel = lax.psum(prior_pick, ("grp", "dev")).astype(jnp.bfloat16)
    summed = lax.psum(weight * jnp.dot(my_rows, project, preferred_element_type=jnp.float32), "grp")
    prior_rows = lax.all_gather(prior_panel, "grp", axis=0, tiled=True)
    schur_panel = summed - lax.dot_general(
        prior_rows, prior_sel, (((1,), (1,)), ((), ())), preferred_element_type=jnp.float32
    )
    corner_part = take_rows(schur_panel, selected, member * height, height)
    corner = lax.psum(corner_part, "dev")
    factor = jnp.linalg.cholesky(corner)
    solved = jax.scipy.linalg.solve_triangular(factor, schur_panel.T, lower=True).T
    block_out = mark_rows(solved, selected, member * height)
    panel_block = block_out.astype(jnp.bfloat16)
    panel_out = lax.dynamic_slice_in_dim(block_out, group_index * own_rows, own_rows, 0)
    products = lax.dot_general(
        my_rows, panel_block, (((0,), (0,)), ((), ())), preferred_element_type=jnp.float32
    ) / math.sqrt(N1)
    residual = lax.psum_scatter(products, "dev", scatter_dimension=0, tiled=True)
    return (panel_out, residual[None])


def solution(mesh):
    return jax.shard_map(
        body,
        mesh=mesh,
        in_specs=(
            P("grp", "dev", None),
            P("grp", None, None),
            P(),
            P(),
            P(),
            P(("dev", "grp"), None),
        ),
        out_specs=(P(("dev", "grp"), None), P("grp", "dev", None)),
        check_vma=False,
    )
```

profile of v0, /device:TPU:1, one launch (start us, length us, event | category | flops | bytes accessed | tf_op | source)
XLA Modules:
  0.0 980.4 jit_solution(14594765991399988502)
XLA Ops:
  8.9 6.0 gather_fusion
  14.9 1.0 select_convert_fusion
  17.3 1.2 fusion.27
  18.5 284.2 %all-reduce.6.cloned.1.call-done = bf16[256,1024]{1,0:T(8,128)(2,1)} async-done(((bf16[256,1024]{1,0:T(8,128)(2,1)}), bf16[256,1024]{1,0:T(8,128)(2,1)}) %all-reduce.6.cloned.1.call-update) | async-done | bytes 524304 | tf_op jit(solution)/shard_map/psum | solution.py:35
  302.7 9.0 fusion.1
  312.6 1.1 gather_fusion.1
  313.9 81.1 %all-reduce.11 = bf16[256,256]{0,1:T(8,128)(2,1)S(1)} all-reduce(f32[256,256]{0,1:T(8,128)S(1)} %convert_select_fusion), channel_id=1, replica_groups=mesh['grp'=8,'dev'=32] {'grp','dev'}, use_global_device_ids=true, to_apply=%region_5.6 | all-reduce | flops 65536 | bytes 393216 | tf_op jit(solution)/shard_map/psum | solution.py:41
  395.0 104.4 %all-reduce.8.cloned.1.call-done = f32[4096,256]{0,1:T(8,128)} async-done(((f32[4096,256]{0,1:T(8,128)}), f32[4096,256]{0,1:T(8,128)}) %all-reduce.8.cloned.1.call-update) | async-done | bytes 4194320 | tf_op jit(solution)/shard_map/psum | solution.py:42
  499.5 5.5 fusion
  505.0 5.6 copy.29
  510.6 3.2 gather_fusion.2
  514.9 1.3 compare_reduce_fusion
  516.2 269.5 %all-reduce.10.cloned.1.call-done = f32[256,256]{0,1:T(8,128)} async-done(((f32[256,256]{0,1:T(8,128)}), f32[256,256]{0,1:T(8,128)}) %all-reduce.10.cloned.1.call-update) | async-done | bytes 262160 | tf_op jit(solution)/shard_map/psum | solution.py:48
  785.7 1.1 copy.31
  786.8 1.0 fusion.19
  787.8 11.7 %cholesky.48 = f32[128,128]{1,0:T(8,128)S(1)} custom-call(f32[128,128]{1,0:T(8,128)S(1)} %cholesky.112), custom_call_target="Cholesky" | custom-call | tf_op jit(solution)/shard_map/jit(cholesky)/cholesky | solution.py:49
  799.6 9.8 %custom-call.15 = f32[1,128,128]{1,2,0:T(8,128)S(1)} custom-call(f32[1,128,128]{2,1,0:T(8,128)S(1)} %get-tuple-element.43), custom_call_target="InvertDiagBlocksLowerTriangular" | custom-call | tf_op jit(solution)/shard_map/jit(cholesky)/cholesky | solution.py:49
  809.9 11.7 %cholesky.101 = f32[128,128]{1,0:T(8,128)S(1)} custom-call(f32[128,128]{1,0:T(8,128)S(1)} %convolution_subtract_fusion.1), custom_call_target="Cholesky" | custom-call | tf_op jit(solution)/shard_map/jit(cholesky)/cholesky | solution.py:49
  824.0 4.2 while.1
  824.6 1.4 dynamic-slice.12
  826.7 1.4 dynamic-slice.12
  828.2 19.9 %custom-call.16 = f32[2,128,128]{1,2,0:T(8,128)S(1)} custom-call(f32[2,128,128]{2,1,0:T(8,128)S(1)} %get-tuple-element.9), custom_call_target="InvertDiagBlocksLowerTriangular" | custom-call | tf_op jit(solution)/shard_map/jit(_solve_triangular)/triangular_solve | solution.py:50
  848.1 3.7 fusion.2
  851.8 2.0 convolution_subtract_fusion
  853.8 1.9 fusion.22
  856.2 1.9 copy-done.3
  858.1 2.4 fusion.11
  860.5 1.3 copy.38
  861.8 1.1 dynamic-slice_bitcast_fusion
  862.9 1.0 copy.36
  863.9 107.8 %reduce-scatter.4.cloned.1.call-done = f32[32,256]{1,0:T(8,128)} async-done(((f32[1024,256]{1,0:T(8,128)}), f32[32,256]{1,0:T(8,128)}) %reduce-scatter.4.cloned.1.call-update) | async-done | bytes 32784
  971.7 0.9 copy.39
  (64 shorter events, 8.5 us)
Async XLA Ops:
  8.0 294.7 %copy-start = (bf16[1,1024,1024]{2,1,0:T(8,128)(2,1)S(1)}, bf16[1,1024,1024]{2,1,0:T(8,128)(2,1)}, u32[]{:S(2)}) copy-start(bf16[1,1024,1024]{2,1,0:T(8,128)(2,1)} %param.7) | copy-start | bytes 6291460
  8.0 8.6 copy-start.5
  8.0 9.3 copy-start.6
  8.0 294.7 %all-reduce.6.cloned.1.call-start = ((), (), s32[]{:S(2)}) async-start(), calls=%async_computation.1 | async-start | bytes 1048576 | tf_op jit(solution)/shard_map/psum | solution.py:35
  16.0 379.0 %all-gather.2.cloned.1.call-start = ((), (), s32[]{:S(2)}) async-start(), calls=%async_computation.3 | async-start | bytes 2359296 | tf_op jit(solution)/shard_map/all_gather | solution.py:43
  16.6 482.9 %all-reduce.8.cloned.1.call-start = ((), (), s32[]{:S(2)}) async-start(), calls=%async_computation.2 | async-start | bytes 8388608 | tf_op jit(solution)/shard_map/psum | solution.py:42
  311.7 0.9 copy-start.2
  311.7 474.0 %all-reduce.10.cloned.1.call-start = ((), (), s32[]{:S(2)}) async-start(), calls=%async_computation.4 | async-start | bytes 524288 | tf_op jit(solution)/shard_map/psum | solution.py:48
  505.0 9.9 %copy-start.4 = (s32[256]{0:T(256)S(1)}, s32[256]{0:T(256)}, u32[]{:S(2)}) copy-start(s32[256]{0:T(256)} %param.8) | copy-start | bytes 3076
  514.7 457.1 %reduce-scatter.4.cloned.1.call-start = ((), (), s32[]{:S(2)}) async-start(), calls=%async_computation.5 | async-start | bytes 1081344
  848.1 3.7 copy-start.1
  851.8 6.4 slice-start
  853.7 4.4 slice-start.1
  856.2 1.9 copy-start.3
Sparse Core Ops, SparseCore 0:
  16.1 286.5 all-reduce.5
  514.8 270.8 all-reduce.9
  862.0 109.7 reduce-scatter.3
Sparse Core Ops, SparseCore 1:
  18.3 59.4 all-gather.1
  311.8 187.6 all-reduce.7
where the time goes:
time: 985 us; the launch traced here: 980 us
  waiting for transfers between devices  767 us (78%)
  blocking collectives  81.1 us (8%)
  other arithmetic  61.1 us (6%)
  local copies, waits for them, and re-layouts  29.5 us (3%)
  matrix products  24.9 us (3%)
  between operations  16.8 us (2%)
    psum x1, waiting for transfers between devices, body(): chosen = lax.psum(picked.astype(jnp.bfloat16), 'dev')  284 us
    psum x1, waiting for transfers between devices, body(): corner = lax.psum(corner_part, 'dev')  270 us
    unnamed x6, waiting for transfers between devices  108 us
    psum x1, waiting for transfers between devices, body(): lax.psum(weight * jnp.dot(my_rows, project, preferred_element_type=jnp.fl...  104 us
    psum x1, blocking collectives, body(): prior_sel = lax.psum(prior_pick, ('grp', 'dev')).astype(jnp.bfloat16)  81.1 us
    another operation x6, other arithmetic, body(): factor = jnp.linalg.cholesky(corner)  34 us
    another operation x3, other arithmetic, body(): jax.scipy.linalg.solve_triangular(factor, schur_panel.T, lower=True)  19.9 us
  transfers between devices with their start and end apart: 5, of which 4 were waited for; matrix products, arithmetic and copies ran while one was open for 2% of the time, Pallas kernels for 0%

commit v1 on v0

v1 whole, which is shorter than its diff:
```python
import functools
import math

import jax
import jax.numpy as jnp
from jax import lax
from jax.experimental import pallas as pl
from jax.experimental.pallas import tpu as pltpu
from jax.sharding import PartitionSpec as P

N1 = 131072
MESH = pl.DeviceIdType.MESH
HIGHEST = lax.Precision.HIGHEST
F32 = jnp.float32
BF16 = jnp.bfloat16
LANES = 128
CORES, XHI = 2, 2
TOP = 32767.0


def params(collective_id, limit=60):
    return pltpu.CompilerParams(
        collective_id=collective_id, has_side_effects=True, vmem_limit_bytes=limit << 20
    )


def dot(a, b, ca, cb, precision=None):
    return lax.dot_general(
        a, b, (((ca,), (cb,)), ((), ())), precision=precision, preferred_element_type=F32
    )


def meet(partners):
    barrier = pltpu.get_barrier_semaphore()
    for where in partners:
        pl.semaphore_signal(barrier, inc=1, device_id=where, device_id_type=MESH)
    pl.semaphore_wait(barrier, len(partners))


def remote(src, dst, send, recv, where):
    return pltpu.make_async_remote_copy(
        src_ref=src, dst_ref=dst, send_sem=send, recv_sem=recv, device_id=where, device_id_type=MESH
    )


def dev_partners(grp, dev, count):
    depth = count // (CORES * XHI)
    per = CORES * XHI
    z, rest = dev // per, dev % per
    xhi, core = rest // CORES, rest % CORES
    at = lambda zz, xx, cc: (grp, (zz * XHI + xx) * CORES + cc)
    others = [at((z + o) % depth, xhi, core) for o in range(1, depth)]
    return z, xhi, core, at(z, xhi, 1 - core), at(z, 1 - xhi, core), others


def rows_kernel(
    groups, count, border, prior, sel, out,
    big, flat, got1, got2, got3, load, send1, recv1, send2, recv2, send3, recv3, send4, recv4, send5, recv5, send6, recv6,
):
    grp, dev = lax.axis_index("grp"), lax.axis_index("dev")
    z, xhi, core, cpart, xpart, zparts = dev_partners(grp, dev, count)
    depth = count // (CORES * XHI)
    pieces, height = big.shape[0], big.shape[1]
    width, own = sel.shape[0], prior.shape[0]
    for i in range(pieces):
        pltpu.make_async_copy(border.at[pl.ds(i * height, height)], big.at[i], load.at[i]).start()
    meet([cpart, xpart] + zparts)
    want = sel[...][:, :1]
    first = (dev * groups + grp) * own
    hot = (want - first == lax.broadcasted_iota(jnp.int32, (width, own), 1)).astype(F32).astype(BF16)
    total = flat.shape[0]
    cols = (total - 2 * width) // width
    mine = dot(hot, prior[...], 1, 0).astype(BF16)
    for c in range(2):
        flat[pl.ds((cols + c) * width, width), :] = mine[:, c * LANES : (c + 1) * LANES]
    acc = None
    for i in range(pieces):
        pltpu.make_async_copy(border.at[pl.ds(i * height, height)], big.at[i], load.at[i]).wait()
        base = dev * (pieces * height) + i * height
        hot = (want - base == lax.broadcasted_iota(jnp.int32, (width, height), 1)).astype(F32).astype(BF16)
        part = dot(hot, big[i], 1, 0)
        acc = part if acc is None else acc + part
    acc = acc.astype(BF16)
    for c in range(cols):
        flat[pl.ds(c * width, width), :] = acc[:, c * LANES : (c + 1) * LANES]
    half, quarter, part = total // CORES, total // (CORES * XHI), total // count
    go = remote(flat.at[pl.ds((1 - core) * half, half)], got1, send1, recv1, cpart)
    go.start()
    go.wait()
    at1 = core * half
    flat[pl.ds(at1, half), :] = flat[pl.ds(at1, half), :] + got1[...]
    go = remote(flat.at[pl.ds(at1 + (1 - xhi) * quarter, quarter)], got2, send2, recv2, xpart)
    go.start()
    go.wait()
    at2 = at1 + xhi * quarter
    flat[pl.ds(at2, quarter), :] = flat[pl.ds(at2, quarter), :] + got2[...]
    gos = []
    for o in range(1, depth):
        there = (z + o) % depth
        go = remote(flat.at[pl.ds(at2 + there * part, part)], got3.at[o - 1], send3.at[o - 1], recv3.at[o - 1], zparts[o - 1])
        go.start()
        gos.append(go)
    at3 = at2 + z * part
    value = flat[pl.ds(at3, part), :]
    for o in range(1, depth):
        gos[o - 1].wait_recv()
        value = value + got3[o - 1]
    out[pl.ds(at3, part), :] = value
    outs = []
    for o in range(1, depth):
        go = remote(out.at[pl.ds(at3, part)], out.at[pl.ds(at3, part)], send4.at[o - 1], recv4.at[o - 1], zparts[o - 1])
        go.start()
        outs.append(go)
    for o in range(1, depth):
        there = at2 + ((z + depth - o) % depth) * part
        remote(out.at[pl.ds(there, part)], out.at[pl.ds(there, part)], send4.at[o - 1], recv4.at[o - 1], zparts[o - 1]).wait_recv()
    go = remote(out.at[pl.ds(at2, quarter)], out.at[pl.ds(at2, quarter)], send5, recv5, xpart)
    go.start()
    outs.append(go)
    other = at1 + (1 - xhi) * quarter
    remote(out.at[pl.ds(other, quarter)], out.at[pl.ds(other, quarter)], send5, recv5, xpart).wait_recv()
    go = remote(out.at[pl.ds(at1, half)], out.at[pl.ds(at1, half)], send6, recv6, cpart)
    go.start()
    outs.append(go)
    other = (1 - core) * half
    remote(out.at[pl.ds(other, half)], out.at[pl.ds(other, half)], send6, recv6, cpart).wait_recv()
    for go in gos + outs:
        go.wait_send()


def rows_call(groups, count, border, prior, sel):
    rows, size = border.shape
    width = sel.shape[0]
    total = (size // LANES + 2) * width
    depth = count // (CORES * XHI)
    height = min(512, rows)
    dma = pltpu.SemaphoreType.DMA
    vm = pl.BlockSpec(memory_space=pltpu.VMEM)
    n = max(depth - 1, 1)
    return pl.pallas_call(
        functools.partial(rows_kernel, groups, count),
        out_shape=jax.ShapeDtypeStruct((total, LANES), BF16),
        in_specs=[pl.BlockSpec(memory_space=pl.ANY), vm, vm],
        out_specs=vm,
        scratch_shapes=[
            pltpu.VMEM((rows // height, height, size), BF16),
            pltpu.VMEM((total, LANES), BF16),
            pltpu.VMEM((total // CORES, LANES), BF16),
            pltpu.VMEM((total // (CORES * XHI), LANES), BF16),
            pltpu.VMEM((n, total // count, LANES), BF16),
            dma((rows // height,)),
            dma, dma, dma, dma, dma((n,)), dma((n,)), dma((n,)), dma((n,)), dma, dma, dma, dma,
        ],
        compiler_params=params(0),
        name="rows",
    )(border, prior, sel)


def refine(d):
    r = 1.0 / d
    return r * (2.0 - d * r)


def eliminate(work, inv):
    size = work.shape[0]
    lane = lax.broadcasted_iota(jnp.int32, (8, 2 * size), 1)
    row = lax.broadcasted_iota(jnp.int32, (8, 2 * size), 0)

    def panel(p, carry):
        at = pl.multiple_of(p * 8, 8)
        block = work[pl.ds(at, 8), :]
        near = pltpu.roll(block, (2 * size - at) % (2 * size), axis=1)
        cs = [jnp.broadcast_to(near[:, j : j + 1], (8, 2 * size)) for j in range(8)]
        pivots = jnp.zeros((8, 2 * size), F32)
        for j in range(8):
            pivots = jnp.where(row == j, cs[j], pivots)
            d = jnp.broadcast_to(cs[j][j : j + 1, :], (8, 2 * size))
            m = jnp.where(row > j, cs[j] * refine(d), 0.0)
            block = block - m * jnp.broadcast_to(block[j : j + 1, :], (8, 2 * size))
            for k in range(j + 1, 8):
                cs[k] = cs[k] - m * jnp.broadcast_to(cs[k][j : j + 1, :], (8, 2 * size))
        r = lax.rsqrt(pivots)
        r = r * (1.5 - 0.5 * pivots * r * r)
        inv[pl.ds(at, 8), :] = (block * r)[:, size:]
        scaled = jnp.where((lane >= at + 8) & (lane < size), block * refine(pivots), 0.0)
        turned = jnp.transpose(scaled)[:size, :]
        rest = work[...]
        for j in range(8):
            rest = rest - jnp.broadcast_to(turned[:, j : j + 1], rest.shape) * jnp.broadcast_to(block[j : j + 1, :], rest.shape)
        work[...] = rest
        return carry

    lax.fori_loop(0, size // 8, panel, 0)


def inverse_factor(a, work, inv):
    n = a.shape[0]
    base = work.shape[0]
    if n == base:
        i = lax.broadcasted_iota(jnp.int32, (n, n), 0)
        j = lax.broadcasted_iota(jnp.int32, (n, n), 1)
        work[...] = jnp.concatenate([a, (i == j).astype(F32)], axis=1)
        eliminate(work, inv)
        return inv[...]
    h = n // 2
    w11 = inverse_factor(a[:h, :h], work, inv)
    l21 = dot(a[h:, :h], w11, 1, 1, HIGHEST)
    w22 = inverse_factor(a[h:, h:] - dot(l21, l21, 1, 1, HIGHEST), work, inv)
    w21 = -dot(dot(w22, l21, 1, 0, HIGHEST), w11, 1, 0, HIGHEST)
    top = jnp.concatenate([w11, jnp.zeros((h, h), F32)], axis=1)
    return jnp.concatenate([top, jnp.concatenate([w21, w22], axis=1)], axis=0)


def schur_kernel(
    groups, border, inverse, flat, prior, sel, asg, prob, panel, rounded,
    big, minv, fl, picked, project, corner, corner_got, corner_sum, q_got, q, code, code_got, scale, scale_got, work, invb,
    load, send, recv,
):
    grp, dev = lax.axis_index("grp"), lax.axis_index("dev")
    order = [o for o in (5, 7, 3, 4, 1, 6, 2) if o < groups]
    parts = {o: (grp ^ o, dev) for o in order}
    width = picked.shape[0]
    size = picked.shape[1]
    own = prior.shape[0]
    loads = [
        pltpu.make_async_copy(flat, fl, load.at[groups]),
        pltpu.make_async_copy(inverse, minv, load.at[groups + 1]),
    ] + [
        pltpu.make_async_copy(border.at[pl.ds((grp ^ o) * own, own)], big.at[o], load.at[o])
        for o in order + [0]
    ]
    for go in loads:
        go.start()
    meet([parts[o] for o in order])
    scenario = asg[grp]
    weight = 0.0
    for i in range(groups):
        weight = weight + jnp.where(scenario == i, prob[i], 0.0)
    loads[0].wait()
    for c in range(size // LANES):
        picked[:, c * LANES : (c + 1) * LANES] = fl[pl.ds(c * width, width), :]
    qbase = (size // LANES) * width
    gos = []

    def go_to(kind, o, src, dst):
        go = remote(src, dst, send.at[kind, o - 1], recv.at[kind, o - 1], parts[o])
        go.start()
        gos.append(go)

    def landed(kind, o, dst):
        remote(dst, dst, send.at[kind, o - 1], recv.at[kind, o - 1], parts[o]).wait_recv()

    qpart = (2 * width) // groups
    for o in order:
        go_to(0, o, fl.at[pl.ds(qbase + (grp ^ o) * qpart, qpart)], q_got.at[o])
    loads[1].wait()
    project[...] = dot(minv[...], picked[...], 1, 1).astype(BF16)
    corner[...] = weight * dot(picked[...], project[...], 1, 0)
    cpart = width // groups
    for o in order:
        go_to(1, o, corner.at[pl.ds((grp ^ o) * cpart, cpart)], corner_got.at[o])
    for o in order:
        landed(0, o, q_got.at[o])
    mine = fl[pl.ds(qbase + grp * qpart, qpart), :]
    for o in order:
        mine = mine + q_got[o]
    q[pl.ds(grp * qpart, qpart), :] = mine
    for o in order:
        here = q.at[pl.ds(grp * qpart, qpart)]
        go_to(2, o, here, here)
    first = True
    for n, o in enumerate(order):
        loads[2 + n].wait()
        block = weight * jnp.dot(big[o], project[...], preferred_element_type=F32)
        peak = jnp.maximum(jnp.max(jnp.abs(block), axis=0, keepdims=True), 1e-30)
        x = block * (TOP / peak)
        code[o] = jnp.round(x).astype(jnp.int32).astype(jnp.int16)
        scale[o] = jnp.broadcast_to(peak * (1.0 / TOP), scale.shape[1:])
        go_to(4, o, scale.at[o], scale_got.at[o])
        go_to(5, o, code.at[o], code_got.at[o])
        if first:
            first = False
            for k in order:
                landed(1, k, corner_got.at[k])
            mine = corner[pl.ds(grp * cpart, cpart), :]
            for k in order:
                mine = mine + corner_got[k]
            corner_sum[pl.ds(grp * cpart, cpart), :] = mine
            for k in order:
                here = corner_sum.at[pl.ds(grp * cpart, cpart)]
                go_to(3, k, here, here)
    loads[-1].wait()
    panel[...] = weight * jnp.dot(big[0], project[...], preferred_element_type=F32)
    for o in order:
        there = pl.ds((grp ^ o) * qpart, qpart)
        landed(2, o, q.at[there])
        there = pl.ds((grp ^ o) * cpart, cpart)
        landed(3, o, corner_sum.at[there])
    qs = jnp.concatenate([q[pl.ds(c * width, width), :] for c in range(2)], axis=1)
    a = corner_sum[...] - dot(qs, qs, 1, 1)
    a = 0.5 * (a + jnp.transpose(a))
    w = inverse_factor(a, work, invb)
    total = panel[...] - dot(prior[...], qs, 1, 1)
    for o in order:
        landed(4, o, scale_got.at[o])
        landed(5, o, code_got.at[o])
        total = total + code_got[o].astype(jnp.int32).astype(F32) * scale_got[o][:1, :]
    solved = dot(total, w, 1, 1, HIGHEST)
    ids = (dev * groups + grp) * own + lax.broadcasted_iota(jnp.int32, (own, width), 0)
    hit = jnp.max((ids == sel[...]).astype(F32), axis=1, keepdims=True)
    solved = jnp.where(hit > 0.5, 0.0, solved)
    panel[...] = solved
    rounded[...] = solved.astype(BF16)
    for go in gos:
        go.wait_send()


def schur_call(groups, border, inverse, flat, prior, sel, asg, prob):
    rows, size = border.shape
    own, width = prior.shape
    dma = pltpu.SemaphoreType.DMA
    vm = pl.BlockSpec(memory_space=pltpu.VMEM)
    anyspace = pl.BlockSpec(memory_space=pl.ANY)
    sm = pl.BlockSpec(memory_space=pltpu.SMEM)
    base = 64
    return pl.pallas_call(
        functools.partial(schur_kernel, groups),
        out_shape=(jax.ShapeDtypeStruct((own, width), F32), jax.ShapeDtypeStruct((own, width), BF16)),
        in_specs=[anyspace, anyspace, anyspace, vm, vm, sm, sm],
        out_specs=(vm, vm),
        scratch_shapes=[
            pltpu.VMEM((groups, own, size), BF16),
            pltpu.VMEM((size, size), BF16),
            pltpu.VMEM(flat.shape, BF16),
            pltpu.VMEM((width, size), BF16),
            pltpu.VMEM((size, width), BF16),
            pltpu.VMEM((width, width), F32),
            pltpu.VMEM((groups, width // groups, width), F32),
            pltpu.VMEM((width, width), F32),
            pltpu.VMEM((groups, 2 * width // groups, LANES), BF16),
            pltpu.VMEM((2 * width, LANES), BF16),
            pltpu.VMEM((groups, own, width), jnp.int16),
            pltpu.VMEM((groups, own, width), jnp.int16),
            pltpu.VMEM((groups, 8, width), F32),
            pltpu.VMEM((groups, 8, width), F32),
            pltpu.VMEM((base, 2 * base), F32),
            pltpu.VMEM((base, base), F32),
            dma((groups + 2,)),
            dma((6, groups - 1)),
            dma((6, groups - 1)),
        ],
        compiler_params=params(1),
        name="schur",
    )(border, inverse, flat, prior, sel, asg, prob)


def products_kernel(
    groups, count, border, rounded, out,
    big, panel, acc, sums, got1, keep1, got2, keep2, got3, load, send, recv, send1, recv1, send2, recv2, send3, recv3,
):
    grp, dev = lax.axis_index("grp"), lax.axis_index("dev")
    z, xhi, core, cpart, xpart, zparts = dev_partners(grp, dev, count)
    depth = count // (CORES * XHI)
    order = [o for o in (5, 7, 3, 4, 1, 6, 2) if o < groups]
    own = rounded.shape[0]
    loads = [
        pltpu.make_async_copy(border.at[pl.ds((grp ^ o) * own, own)], big.at[o], load.at[o])
        for o in [0] + order[::-1]
    ]
    for go in loads:
        go.start()
    meet([(grp ^ o, dev) for o in order] + [cpart, xpart] + zparts)
    gos = []
    for o in order:
        go = remote(rounded, panel.at[o], send.at[o - 1], recv.at[o - 1], (grp ^ o, dev))
        go.start()
        gos.append(go)
    loads[0].wait()
    acc[...] = dot(rounded[...], big[0], 0, 0)
    for n, o in enumerate(order[::-1]):
        loads[1 + n].wait()
        gos[len(order) - 1 - n].wait_recv()
        acc[...] += dot(panel[o], big[o], 0, 0)
    width = acc.shape[0]
    piece = sums.shape[3]
    scale = 1.0 / math.sqrt(N1)
    for e in range(acc.shape[1] // LANES):
        turned = jnp.transpose(acc[:, e * LANES : (e + 1) * LANES]) * scale
        for k in range(LANES // piece):
            at = e * (LANES // piece) + k
            zz, xx, cc = at // (XHI * CORES), (at // CORES) % XHI, at % CORES
            sums[cc, zz, xx] = turned[k * piece : (k + 1) * piece, :]
    go = remote(sums.at[1 - core], got1, send1, recv1, cpart)
    go.start()
    gos.append(go)
    go.wait_recv()
    for x in range(XHI):
        for zz in range(depth):
            keep1[x, zz] = sums[core, zz, x] + got1[zz, x]
    go = remote(keep1.at[1 - xhi], got2, send2, recv2, xpart)
    go.start()
    gos.append(go)
    go.wait_recv()
    keep2[...] = keep1[xhi] + got2[...]
    last = []
    for o in range(1, depth):
        go = remote(keep2.at[(z + o) % depth], got3.at[o - 1], send3.at[o - 1], recv3.at[o - 1], zparts[o - 1])
        go.start()
        last.append(go)
    value = keep2[z]
    for o in range(1, depth):
        last[o - 1].wait_recv()
        value = value + got3[o - 1]
    out[...] = value
    for go in gos + last:
        go.wait_send()


def products_call(groups, count, border, rounded):
    rows, size = border.shape
    own, width = rounded.shape
    piece = size // count
    depth = count // (CORES * XHI)
    n = max(depth - 1, 1)
    dma = pltpu.SemaphoreType.DMA
    vm = pl.BlockSpec(memory_space=pltpu.VMEM)
    return pl.pallas_call(
        functools.partial(products_kernel, groups, count),
        out_shape=jax.ShapeDtypeStruct((piece, width), F32),
        in_specs=[pl.BlockSpec(memory_space=pl.ANY), vm],
        out_specs=vm,
        scratch_shapes=[
            pltpu.VMEM((groups, own, size), BF16),
            pltpu.VMEM((groups, own, width), BF16),
            pltpu.VMEM((width, size), F32),
            pltpu.VMEM((CORES, depth, XHI, piece, width), F32),
            pltpu.VMEM((depth, XHI, piece, width), F32),
            pltpu.VMEM((XHI, depth, piece, width), F32),
            pltpu.VMEM((depth, piece, width), F32),
            pltpu.VMEM((depth, piece, width), F32),
            pltpu.VMEM((n, piece, width), F32),
            dma((groups,)), dma((groups - 1,)), dma((groups - 1,)), dma, dma, dma, dma, dma((n,)), dma((n,)),
        ],
        compiler_params=params(2),
        name="products",
    )(border, rounded)


def body(border, inverse_blocks, selected, assignment, probability, prior_panel):
    groups, count = lax.axis_size("grp"), lax.axis_size("dev")
    mine = border[0]
    column = jnp.broadcast_to(selected[:, None], (selected.shape[0], LANES))
    flat = rows_call(groups, count, mine, prior_panel, column)
    panel, rounded = schur_call(
        groups, mine, inverse_blocks[0], flat, prior_panel, selected[None, :], assignment, probability
    )
    residual = products_call(groups, count, mine, rounded)
    return (panel, residual[None])


def solution(mesh):
    return jax.shard_map(
        body,
        mesh=mesh,
        in_specs=(
            P("grp", "dev", None),
            P("grp", None, None),
            P(),
            P(),
            P(),
            P(("dev", "grp"), None),
        ),
        out_specs=(P(("dev", "grp"), None), P("grp", "dev", None)),
        check_vma=False,
    )
```

time: 985 us -> 160 us (0.16)
  the two profiles are of different devices: /device:TPU:1 before, /device:TPU:8 now
where the time goes in v1:
time: 160 us
  Pallas kernels  155 us (97%)
  local copies, waits for them, and re-layouts  3.61 us (2%)
    pallas_call x1, Pallas kernels, products_call(): pl.pallas_call(functools.partial(products_kernel, groups, count), out_sha...  59.1 us
    pallas_call x1, Pallas kernels, schur_call(): pl.pallas_call(functools.partial(schur_kernel, groups), out_shape=(jax.Sh...  57.4 us
    pallas_call x1, Pallas kernels, rows_call(): pl.pallas_call(functools.partial(rows_kernel, groups, count), out_shape=j...  38.8 us

profile of v1, /device:TPU:8, one launch (start us, length us, event | category | flops | bytes accessed | tf_op | source)
XLA Modules:
  0.0 159.7 jit_solution(8842718197750563672)
XLA Ops:
  0.6 1.4 broadcast_in_dim.12.sel
  2.1 38.8 %rows.1.flat = bf16[2560,128]{1,0:T(8,128)(2,1)} custom-call(bf16[4096,1024]{1,0:T(8,128)(2,1)} %bitcast.4, bf16[512,256]{1,0:T(8,128)(2,1)} %prior.3, s32[256,128]{1,0:T(8,128)} %broadcast_in_dim.12.sel), custom_call_target="tpu_custom_call" | custom-call | tf_op jit(solution)/shard_map/rows/pallas_call | solution.py:140
  40.8 57.4 %schur.1 = (f32[512,256]{1,0:T(8,128)}, bf16[512,256]{1,0:T(8,128)(2,1)}) custom-call(bf16[4096,1024]{1,0:T(8,128)(2,1)} %bitcast.5, bf16[1024,1024]{1,0:T(8,128)(2,1)} %bitcast.7, bf16[2560,128]{1,0:T(8,128)(2,1)} %rows.1.flat, bf16[512,256]{1,0:T(8,128)(2,1)} %prior.3, s32[1,256]{1,0:T(1,128)} %bitcast.9, s32[8]{0:T(128)} %asg.1, f32[8]{0:T(128)} %prob.1), custom_call_target="tpu_custom_call" | custom-call | tf_op jit(solution)/shard_map/schur/pallas_call | solution.py:326
  98.3 0.0 copy-start
  98.3 59.1 %products.1 = f32[32,256]{1,0:T(8,128)} custom-call(bf16[4096,1024]{1,0:T(8,128)(2,1)} %bitcast.6, bf16[512,256]{1,0:T(8,128)(2,1)} %get-tuple-element.5.rounded), custom_call_target="tpu_custom_call" | custom-call | tf_op jit(solution)/shard_map/products/pallas_call | solution.py:427
  157.5 0.0 copy-done
  157.5 0.8 copy.10
  158.3 1.4 copy.11
Async XLA Ops:
  98.3 59.2 %copy-start = (f32[512,256]{1,0:T(8,128)S(1)}, f32[512,256]{1,0:T(8,128)}, u32[]{:S(2)}) copy-start(f32[512,256]{1,0:T(8,128)} %get-tuple-element.8) | copy-start | bytes 1572868

commit v2 on v0

v2 whole, which is shorter than its diff:
```python
import functools
import math

import jax
import jax.numpy as jnp
from jax import lax
from jax.experimental import pallas as pl
from jax.experimental.pallas import tpu as pltpu
from jax.sharding import PartitionSpec as P

N1 = 131072
MESH = pl.DeviceIdType.MESH
HIGHEST = lax.Precision.HIGHEST
F32 = jnp.float32
BF16 = jnp.bfloat16
I16 = jnp.int16
LANES = 128
CORES, XHI, XLO = 2, 2, 2
TOP = 32767.0
BASE = 64


def dot(a, b, ca, cb, precision=None):
    return lax.dot_general(
        a, b, (((ca,), (cb,)), ((), ())), precision=precision, preferred_element_type=F32
    )


def split(own, share):
    part = max(16, int(own * share / 16 + 0.5) * 16)
    return own - part, part


def encode(x, code, scale):
    peak = jnp.maximum(jnp.max(jnp.abs(x), axis=0, keepdims=True), 1e-30)
    code[...] = jnp.round(x * (TOP / peak)).astype(jnp.int32).astype(I16)
    scale[...] = peak * (1.0 / TOP)


def decode(code, scale):
    return code.astype(jnp.int32).astype(F32) * scale


def refine(d):
    r = 1.0 / d
    return r * (2.0 - d * r)


def eliminate(work, inv):
    size = work.shape[0]
    lane = lax.broadcasted_iota(jnp.int32, (8, 2 * size), 1)
    row = lax.broadcasted_iota(jnp.int32, (8, 2 * size), 0)

    def panel(p, carry):
        at = pl.multiple_of(p * 8, 8)
        block = work[pl.ds(at, 8), :]
        near = pltpu.roll(block, (2 * size - at) % (2 * size), axis=1)
        cs = [jnp.broadcast_to(near[:, j : j + 1], (8, 2 * size)) for j in range(8)]
        pivots = jnp.zeros((8, 2 * size), F32)
        for j in range(8):
            pivots = jnp.where(row == j, cs[j], pivots)
            d = jnp.broadcast_to(cs[j][j : j + 1, :], (8, 2 * size))
            m = jnp.where(row > j, cs[j] * refine(d), 0.0)
            block = block - m * jnp.broadcast_to(block[j : j + 1, :], (8, 2 * size))
            for k in range(j + 1, 8):
                cs[k] = cs[k] - m * jnp.broadcast_to(cs[k][j : j + 1, :], (8, 2 * size))
        r = lax.rsqrt(pivots)
        r = r * (1.5 - 0.5 * pivots * r * r)
        inv[pl.ds(at, 8), :] = (block * r)[:, size:]
        scaled = jnp.where((lane >= at + 8) & (lane < size), block * refine(pivots), 0.0)
        turned = jnp.transpose(scaled)[:size, :]
        rest = work[...]
        for j in range(8):
            rest = rest - jnp.broadcast_to(turned[:, j : j + 1], rest.shape) * jnp.broadcast_to(block[j : j + 1, :], rest.shape)
        work[...] = rest
        return carry

    lax.fori_loop(0, size // 8, panel, 0)


def inverse_factor(a, work, inv, hooks):
    n = a.shape[0]
    if n == BASE:
        i = lax.broadcasted_iota(jnp.int32, (n, n), 0)
        j = lax.broadcasted_iota(jnp.int32, (n, n), 1)
        work[...] = jnp.concatenate([a, (i == j).astype(F32)], axis=1)
        eliminate(work, inv)
        if hooks:
            hooks.pop(0)()
        return inv[...]
    h = n // 2
    w11 = inverse_factor(a[:h, :h], work, inv, hooks)
    l21 = dot(a[h:, :h], w11, 1, 1, HIGHEST)
    w22 = inverse_factor(a[h:, h:] - dot(l21, l21, 1, 1, HIGHEST), work, inv, hooks)
    w21 = -dot(dot(w22, l21, 1, 0, HIGHEST), w11, 1, 0, HIGHEST)
    top = jnp.concatenate([w11, jnp.zeros((h, h), F32)], axis=1)
    return jnp.concatenate([top, jnp.concatenate([w21, w22], axis=1)], axis=0)


class Mail:
    def __init__(self, send, recv):
        self.send, self.recv, self.ids, self.started = send, recv, {}, []

    def copy(self, key, src, dst, where):
        k = self.ids.setdefault(key, len(self.ids))
        return pltpu.make_async_remote_copy(
            src_ref=src, dst_ref=dst, send_sem=self.send.at[k], recv_sem=self.recv.at[k],
            device_id=where, device_id_type=MESH,
        )

    def start(self, key, src, dst, where):
        go = self.copy(key, src, dst, where)
        go.start()
        self.started.append(go)

    def take(self, key, dst, where):
        self.copy(key, dst, dst, where).wait_recv()

    def close(self):
        for go in self.started:
            go.wait_send()


def kernel(
    groups, count, border, inverse, prior_hbm, sel, asg, prob, panel, out,
    big, minv, prior, flat, rows, got1, got2, got3, q0, qg, qs, qh, qx, qz, q, picked, project,
    corner, corner_got, corner_sum, ya, ya_s, ya_g, ya_sg, xb, xb_s, xb_g, xb_sg,
    xa, xa_s, xa_g, xa_sg, yb, yb_s, yb_g, yb_sg, keep0, keep_a, keep_b, hit, work, invb,
    pan, acc, sums, core_got, keep1, x_code, x_scale, x_got, x_sgot, keep2, z_code, z_scale, z_got, z_sgot,
    load, send, recv,
):
    grp, dev = lax.axis_index("grp"), lax.axis_index("dev")
    depth = count // (CORES * XHI)
    z, xhi, core = dev // (CORES * XHI), (dev // CORES) % XHI, dev % CORES
    at = lambda zz, xx, cc: (grp, (zz * XHI + xx) * CORES + cc)
    cpart, xpart = at(z, xhi, 1 - core), at(z, 1 - xhi, core)
    zparts = {o: at((z + o) % depth, xhi, core) for o in range(1, depth)}
    ys = [y for y in (2, 1, 3) if y < groups // XLO]
    near = [o for o in (5, 4, 7, 6, 3, 2, 1) if o < groups]
    peer = {o: (grp ^ o, dev) for o in near}
    width, size = picked.shape
    own = prior.shape[0]
    mail = Mail(send, recv)

    loads = {o: pltpu.make_async_copy(border.at[pl.ds((grp ^ o) * own, own)], big.at[o], load.at[o]) for o in range(groups)}
    loads["prior"] = pltpu.make_async_copy(prior_hbm, prior, load.at[groups])
    loads["inverse"] = pltpu.make_async_copy(inverse, minv, load.at[groups + 1])
    for name in ["prior"] + list(range(groups)) + ["inverse"]:
        loads[name].start()
    barrier = pltpu.get_barrier_semaphore()
    partners = [cpart, xpart] + list(zparts.values()) + list(peer.values())
    for where in partners:
        pl.semaphore_signal(barrier, inc=1, device_id=where, device_id_type=MESH)

    want = jnp.transpose(jnp.broadcast_to(sel[...], (LANES, width)))[:, :1]
    want = jnp.broadcast_to(want, (width, own))
    lanes = lax.broadcasted_iota(jnp.int32, (width, own), 1)
    first = (dev * groups + grp) * own
    loads["prior"].wait()
    mine = dot((want - first == lanes).astype(F32).astype(BF16), prior[...], 1, 0).astype(BF16)
    for c in range(2):
        q0[pl.ds(c * width, width), :] = mine[:, c * LANES : (c + 1) * LANES]
    total = None
    for o in range(groups):
        loads[o].wait()
        base = (dev * groups + (grp ^ o)) * own
        part = dot((want - base == lanes).astype(F32).astype(BF16), big[o], 1, 0)
        total = part if total is None else total + part
    total = total.astype(BF16)
    for c in range(size // LANES):
        flat[pl.ds(c * width, width), :] = total[:, c * LANES : (c + 1) * LANES]
    pl.semaphore_wait(barrier, len(partners))

    high = flat.shape[0]
    half, quarter, bit = high // CORES, high // (CORES * XHI), high // count
    qpart = (2 * width) // groups
    qhalf, qquart = qpart // CORES, qpart // (CORES * XHI)
    at1 = core * half
    at2 = at1 + xhi * quarter
    at3 = at2 + z * bit
    mail.start("r1", flat.at[pl.ds((1 - core) * half, half)], got1, cpart)
    for o in near:
        mail.start(("q0", o), q0.at[pl.ds((grp ^ o) * qpart, qpart)], qg.at[o], peer[o])
    mail.take("r1", got1, cpart)
    flat[pl.ds(at1, half), :] = flat[pl.ds(at1, half), :] + got1[...]
    mail.start("r2", flat.at[pl.ds(at1 + (1 - xhi) * quarter, quarter)], got2, xpart)
    ids = first + lax.broadcasted_iota(jnp.int32, (own, width), 0)
    marked = jnp.max((ids == sel[...]).astype(F32), axis=1, keepdims=True)
    hit[...] = jnp.broadcast_to(marked, hit.shape)
    value = q0[pl.ds(grp * qpart, qpart), :]
    for o in near:
        mail.take(("q0", o), qg.at[o], peer[o])
        value = value + qg[o]
    qs[...] = value
    mail.start("q1", qs.at[pl.ds((1 - core) * qhalf, qhalf)], qh, cpart)
    mail.take("r2", got2, xpart)
    flat[pl.ds(at2, quarter), :] = flat[pl.ds(at2, quarter), :] + got2[...]
    for o in range(1, depth):
        mail.start(("r3", o), flat.at[pl.ds(at2 + ((z + o) % depth) * bit, bit)], got3.at[o - 1], zparts[o])
    mail.take("q1", qh, cpart)
    qs[pl.ds(core * qhalf, qhalf), :] = qs[pl.ds(core * qhalf, qhalf), :] + qh[...]
    qat = core * qhalf + xhi * qquart
    mail.start("q2", qs.at[pl.ds(core * qhalf + (1 - xhi) * qquart, qquart)], qx, xpart)
    value = flat[pl.ds(at3, bit), :]
    for o in range(1, depth):
        mail.take(("r3", o), got3.at[o - 1], zparts[o])
        value = value + got3[o - 1]
    rows[pl.ds(at3, bit), :] = value
    here = rows.at[pl.ds(at3, bit)]
    for o in range(1, depth):
        mail.start(("r4", o), here, here, zparts[o])
    mail.take("q2", qx, xpart)
    qs[pl.ds(qat, qquart), :] = qs[pl.ds(qat, qquart), :] + qx[...]
    for o in range(1, depth):
        mail.start(("q3", o), qs.at[pl.ds(qat, qquart)], qz.at[o - 1], zparts[o])
    for o in range(1, depth):
        mail.take(("r4", o), rows.at[pl.ds(at2 + ((z + depth - o) % depth) * bit, bit)], zparts[o])
    here = rows.at[pl.ds(at2, quarter)]
    mail.start("r5", here, here, xpart)
    value = qs[pl.ds(qat, qquart), :]
    for o in range(1, depth):
        mail.take(("q3", o), qz.at[o - 1], zparts[o])
        value = value + qz[o - 1]
    qrow = grp * qpart
    q[pl.ds(qrow + qat, qquart), :] = value
    here = q.at[pl.ds(qrow + qat, qquart)]
    mail.start("q4", here, here, xpart)
    mail.take("r5", rows.at[pl.ds(at1 + (1 - xhi) * quarter, quarter)], xpart)
    here = rows.at[pl.ds(at1, half)]
    mail.start("r6", here, here, cpart)
    mail.take("q4", q.at[pl.ds(qrow + core * qhalf + (1 - xhi) * qquart, qquart)], xpart)
    here = q.at[pl.ds(qrow + core * qhalf, qhalf)]
    mail.start("q5", here, here, cpart)
    mail.take("r6", rows.at[pl.ds((1 - core) * half, half)], cpart)

    for c in range(size // LANES):
        picked[:, c * LANES : (c + 1) * LANES] = rows[pl.ds(c * width, width), :]
    loads["inverse"].wait()
    project[...] = dot(minv[...], picked[...], 1, 1).astype(BF16)
    scenario = asg[grp]
    weight = 0.0
    for i in range(groups):
        weight = weight + jnp.where(scenario == i, prob[i], 0.0)
    corner[...] = weight * dot(picked[...], project[...], 1, 0)
    cpiece = width // groups
    for o in near:
        mail.start(("c1", o), corner.at[pl.ds((grp ^ o) * cpiece, cpiece)], corner_got.at[o], peer[o])
    mail.take("q5", q.at[pl.ds(qrow + (1 - core) * qhalf, qhalf)], cpart)
    here = q.at[pl.ds(qrow, qpart)]
    for o in near:
        mail.start(("q6", o), here, here, peer[o])

    ra, rb = split(own, 0.6)

    def block(o):
        return weight * jnp.dot(big[o], project[...], preferred_element_type=F32)

    def make(y):
        side = block(2 * y + 1)
        encode(side[ra:], xb.at[y], xb_s.at[y])
        if y:
            encode(side[:ra], ya.at[y, 1], ya_s.at[y, 1])
            same = block(2 * y)
            encode(same[:ra], ya.at[y, 0], ya_s.at[y, 0])
            keep_b[y] = same[ra:]
        else:
            keep_a[...] = side[:ra]

    def ship(y):
        mail.start(("xbs", y), xb_s.at[y], xb_sg.at[y], peer[1])
        mail.start(("xb", y), xb.at[y], xb_g.at[y], peer[1])
        if y:
            mail.start(("yas", y), ya_s.at[y], ya_sg.at[y], peer[2 * y])
            mail.start(("ya", y), ya.at[y], ya_g.at[y], peer[2 * y])

    early = ys[:2]
    for y in early:
        make(y)
    value = corner[pl.ds(grp * cpiece, cpiece), :]
    for o in near:
        mail.take(("c1", o), corner_got.at[o], peer[o])
        value = value + corner_got[o]
    corner_sum[pl.ds(grp * cpiece, cpiece), :] = value
    here = corner_sum.at[pl.ds(grp * cpiece, cpiece)]
    for o in near:
        mail.start(("c2", o), here, here, peer[o])
    for y in early:
        ship(y)
    for y in ys[2:] + [0]:
        make(y)
        ship(y)
    for o in near:
        mail.take(("q6", o), q.at[pl.ds((grp ^ o) * qpart, qpart)], peer[o])
    picks = jnp.concatenate([q[pl.ds(c * width, width), :] for c in range(2)], axis=1)
    keep0[...] = block(0) - dot(prior[...], picks, 1, 1)
    less = dot(picks, picks, 1, 1)
    for o in near:
        mail.take(("c2", o), corner_sum.at[pl.ds((grp ^ o) * cpiece, cpiece)], peer[o])
    a = corner_sum[...] - less
    a = 0.5 * (a + jnp.transpose(a))

    def onward(y):
        mail.take(("xbs", y), xb_sg.at[y], peer[1])
        mail.take(("xb", y), xb_g.at[y], peer[1])
        encode(keep_b[y] + decode(xb_g[y], xb_sg[y]), yb.at[y], yb_s.at[y])
        mail.start(("ybs", y), yb_s.at[y], yb_sg.at[y], peer[2 * y])
        mail.start(("yb", y), yb.at[y], yb_g.at[y], peer[2 * y])

    def across():
        value, here = keep_a[...], keep0[:ra, :]
        for y in ys:
            mail.take(("yas", y), ya_sg.at[y], peer[2 * y])
            mail.take(("ya", y), ya_g.at[y], peer[2 * y])
            value = value + decode(ya_g[y, 1], ya_sg[y, 1])
            here = here + decode(ya_g[y, 0], ya_sg[y, 0])
        encode(value, xa, xa_s)
        mail.start("xas", xa_s, xa_sg, peer[1])
        mail.start("xa", xa, xa_g, peer[1])
        keep0[:ra, :] = here

    steps = [functools.partial(onward, y) for y in ys[:2]]
    hooks = [lambda: [f() for f in steps[:1]], lambda: [f() for f in steps[1:] + [across]], lambda: [onward(y) for y in ys[2:]]]
    w = inverse_factor(a, work, invb, hooks)

    mail.take("xas", xa_sg, peer[1])
    mail.take("xa", xa_g, peer[1])
    mail.take(("xbs", 0), xb_sg.at[0], peer[1])
    mail.take(("xb", 0), xb_g.at[0], peer[1])
    upper = keep0[:ra, :] + decode(xa_g[...], xa_sg[...])
    lower = keep0[ra:, :] + decode(xb_g[0], xb_sg[0])
    for y in ys:
        mail.take(("ybs", y), yb_sg.at[y], peer[2 * y])
        mail.take(("yb", y), yb_g.at[y], peer[2 * y])
        lower = lower + decode(yb_g[y], yb_sg[y])
    solved = dot(jnp.concatenate([upper, lower], axis=0), w, 1, 1, HIGHEST)
    solved = jnp.where(hit[...] > 0.5, 0.0, solved)
    panel[...] = solved
    pan[0] = solved.astype(BF16)

    pa, pb = split(own, 0.4)
    top, low = pl.ds(0, pa), pl.ds(pa, pb)
    mail.start("g1", pan.at[0, low], pan.at[1, low], peer[1])
    for y in ys:
        mail.start(("g2", y), pan.at[0, top], pan.at[2 * y, top], peer[2 * y])
    mail.start("g3", pan.at[0, top], pan.at[1, top], peer[1])
    for y in ys:
        mail.start(("g4", y), pan.at[0, low], pan.at[2 * y, low], peer[2 * y])
    acc[...] = dot(pan[0], big[0], 0, 0)
    mail.take("g1", pan.at[1, low], peer[1])
    for y in ys:
        mail.start(("g5", y), pan.at[1, low], pan.at[2 * y + 1, low], peer[2 * y])
    for y in ys[1:] + ys[:1]:
        mail.take(("g2", y), pan.at[2 * y, top], peer[2 * y])
        mail.start(("g6", y), pan.at[2 * y, top], pan.at[2 * y + 1, top], peer[1])
    mail.take("g3", pan.at[1, top], peer[1])
    acc[...] += dot(pan[1], big[1], 0, 0)
    for y in ys[1:] + ys[:1]:
        mail.take(("g4", y), pan.at[2 * y, low], peer[2 * y])
        acc[...] += dot(pan[2 * y], big[2 * y], 0, 0)
    for y in ys[1:] + ys[:1]:
        mail.take(("g5", y), pan.at[2 * y + 1, low], peer[2 * y])
        mail.take(("g6", y), pan.at[2 * y + 1, top], peer[1])
        acc[...] += dot(pan[2 * y + 1], big[2 * y + 1], 0, 0)

    piece = sums.shape[3]
    scale = 1.0 / math.sqrt(N1)
    for e in range(acc.shape[1] // LANES):
        turned = jnp.transpose(acc[:, e * LANES : (e + 1) * LANES]) * scale
        for k in range(LANES // piece):
            n = e * (LANES // piece) + k
            zz, xx, cc = n // (XHI * CORES), (n // CORES) % XHI, n % CORES
            sums[cc, xx, zz] = turned[k * piece : (k + 1) * piece, :]
    mail.start("s1", sums.at[1 - core], core_got, cpart)
    mail.take("s1", core_got, cpart)
    keep1[...] = (sums[core] + core_got[...]).reshape(keep1.shape)
    encode(keep1[1 - xhi], x_code, x_scale)
    mail.start("s2s", x_scale, x_sgot, xpart)
    mail.start("s2", x_code, x_got, xpart)
    mail.take("s2s", x_sgot, xpart)
    mail.take("s2", x_got, xpart)
    value = keep1[xhi] + decode(x_got[...], x_sgot[...])
    keep2[...] = value.reshape(keep2.shape)
    peak = jnp.maximum(jnp.max(jnp.abs(value), axis=0, keepdims=True), 1e-30)
    z_scale[...] = peak * (1.0 / TOP)
    z_code[...] = jnp.round(value * (TOP / peak)).astype(jnp.int32).astype(I16).reshape(z_code.shape)
    for o in range(1, depth):
        mail.start(("s3s", o), z_scale, z_sgot.at[o - 1], zparts[o])
        mail.start(("s3", o), z_code.at[(z + o) % depth], z_got.at[o - 1], zparts[o])
    value = keep2[z]
    for o in range(1, depth):
        mail.take(("s3s", o), z_sgot.at[o - 1], zparts[o])
        mail.take(("s3", o), z_got.at[o - 1], zparts[o])
        value = value + decode(z_got[o - 1], z_sgot[o - 1])
    out[...] = value
    mail.close()
    assert len(mail.ids) <= send.shape[0], len(mail.ids)


def call(groups, count, border, inverse, prior, sel, asg, prob):
    size = border.shape[1]
    own, width = prior.shape
    depth = count // (CORES * XHI)
    n = max(depth - 1, 1)
    piece = size // count
    high = size // LANES * width
    qpart = 2 * width // groups
    ny = groups // XLO
    ra, rb = split(own, 0.6)
    dma, vmem = pltpu.SemaphoreType.DMA, pltpu.VMEM
    vm = pl.BlockSpec(memory_space=vmem)
    anyspace = pl.BlockSpec(memory_space=pl.ANY)
    sm = pl.BlockSpec(memory_space=pltpu.SMEM)
    return pl.pallas_call(
        functools.partial(kernel, groups, count),
        out_shape=(jax.ShapeDtypeStruct((own, width), F32), jax.ShapeDtypeStruct((piece, width), F32)),
        in_specs=[anyspace, anyspace, anyspace, vm, sm, sm],
        out_specs=(vm, vm),
        scratch_shapes=[
            vmem((groups, own, size), BF16),
            vmem((size, size), BF16),
            vmem((own, width), BF16),
            vmem((high, LANES), BF16),
            vmem((high, LANES), BF16),
            vmem((high // CORES, LANES), BF16),
            vmem((high // (CORES * XHI), LANES), BF16),
            vmem((n, high // count, LANES), BF16),
            vmem((2 * width, LANES), BF16),
            vmem((groups, qpart, LANES), BF16),
            vmem((qpart, LANES), BF16),
            vmem((qpart // CORES, LANES), BF16),
            vmem((qpart // (CORES * XHI), LANES), BF16),
            vmem((n, qpart // (CORES * XHI), LANES), BF16),
            vmem((2 * width, LANES), BF16),
            vmem((width, size), BF16),
            vmem((size, width), BF16),
            vmem((width, width), F32),
            vmem((groups, width // groups, width), F32),
            vmem((width, width), F32),
            vmem((ny, 2, ra, width), I16),
            vmem((ny, 2, 1, width), F32),
            vmem((ny, 2, ra, width), I16),
            vmem((ny, 2, 1, width), F32),
            vmem((ny, rb, width), I16),
            vmem((ny, 1, width), F32),
            vmem((ny, rb, width), I16),
            vmem((ny, 1, width), F32),
            vmem((ra, width), I16),
            vmem((1, width), F32),
            vmem((ra, width), I16),
            vmem((1, width), F32),
            vmem((ny, rb, width), I16),
            vmem((ny, 1, width), F32),
            vmem((ny, rb, width), I16),
            vmem((ny, 1, width), F32),
            vmem((own, width), F32),
            vmem((ra, width), F32),
            vmem((ny, rb, width), F32),
            vmem((own, width), F32),
            vmem((BASE, 2 * BASE), F32),
            vmem((BASE, BASE), F32),
            vmem((groups, own, width), BF16),
            vmem((width, size), F32),
            vmem((CORES, XHI, depth, piece, width), F32),
            vmem((XHI, depth, piece, width), F32),
            vmem((XHI, depth * piece, width), F32),
            vmem((depth * piece, width), I16),
            vmem((1, width), F32),
            vmem((depth * piece, width), I16),
            vmem((1, width), F32),
            vmem((depth, piece, width), F32),
            vmem((depth, piece, width), I16),
            vmem((1, width), F32),
            vmem((n, piece, width), I16),
            vmem((n, 1, width), F32),
            dma((groups + 2,)),
            dma((128,)),
            dma((128,)),
        ],
        compiler_params=pltpu.CompilerParams(
            collective_id=0, has_side_effects=True, vmem_limit_bytes=60 << 20
        ),
        name="panel",
    )(border, inverse, prior, sel, asg, prob)


def body(border, inverse_blocks, selected, assignment, probability, prior_panel):
    groups, count = lax.axis_size("grp"), lax.axis_size("dev")
    panel, residual = call(
        groups, count, border[0], inverse_blocks[0], prior_panel, selected[None, :], assignment, probability
    )
    return (panel, residual[None])


def solution(mesh):
    return jax.shard_map(
        body,
        mesh=mesh,
        in_specs=(
            P("grp", "dev", None),
            P("grp", None, None),
            P(),
            P(),
            P(),
            P(("dev", "grp"), None),
        ),
        out_specs=(P(("dev", "grp"), None), P("grp", "dev", None)),
        check_vma=False,
    )
```

time: 985 us -> 115 us (0.12)
  waiting for transfers between devices: 767 us -> 0 us
  Pallas kernels: 0 us -> 110 us
  blocking collectives: 81.1 us -> 0 us
  other arithmetic: 61.1 us -> 0 us
  local copies, waits for them, and re-layouts: 29.5 us -> 3.24 us
  matrix products: 24.9 us -> 0 us
  between operations: 16.8 us -> 0.64 us
    psum x3 -> x0, waiting for transfers between devices: 658 us -> none  [the longest x1 284 us: body(): chosen = lax.psum(picked.astype(jnp.bfloat16), 'dev')]
    pallas_call x0 -> x1, Pallas kernels: none -> 110 us  [call(): pl.pallas_call(functools.partial(kernel, groups, count), out_shape=(jax.S...]
    unnamed x6 -> x0, waiting for transfers between devices: 108 us -> none
    psum x1 -> x0, blocking collectives: 81.1 us -> none  [body(): prior_sel = lax.psum(prior_pick, ('grp', 'dev')).astype(jnp.bfloat16)]
    another operation x9 -> x0, other arithmetic: 53.9 us -> none  [the longest x6 34 us: body(): factor = jnp.linalg.cholesky(corner)]
    dot_general x3 -> x0, matrix products: 16.8 us -> none  [the longest x1 8.95 us: body(): jnp.dot(my_rows, project, preferred_element_type=jnp.float32)]
    gather x5 -> x0, local copies, waits for them, and re-layouts: 10.5 us -> none  [take_rows(): jnp.take(source, jnp.clip(offsets, 0, count - 1), axis=0)]
  transfers between devices with their start and end apart: 5 -> 0, of which waited for: 4 -> 0; matrix products, arithmetic and copies ran while one was open for 2% -> 0% of each run, Pallas kernels for 0% -> 0%
where the time goes in v2:
time: 115 us; the launch traced here: 114 us
  Pallas kernels  110 us (96%)
  local copies, waits for them, and re-layouts  3.24 us (3%)
    pallas_call x1, Pallas kernels, call(): pl.pallas_call(functools.partial(kernel, groups, count), out_shape=(jax.S...  110 us
    unnamed x2, local copies, waits for them, and re-layouts  3.24 us

profile of v2, /device:TPU:1, one launch (start us, length us, event | category | flops | bytes accessed | tf_op | source)
XLA Modules:
  0.0 114.3 jit_solution(1753547842825312690)
XLA Ops:
  0.6 110.4 %panel.1 = (f32[512,256]{1,0:T(8,128)}, f32[32,256]{1,0:T(8,128)}) custom-call(bf16[4096,1024]{1,0:T(8,128)(2,1)} %bitcast.4, bf16[1024,1024]{1,0:T(8,128)(2,1)} %bitcast.5, bf16[512,256]{1,0:T(8,128)(2,1)} %prior_hbm.1, s32[1,256]{1,0:T(1,128)} %bitcast.7, s32[8]{0:T(128)} %asg.1, f32[8]{0:T(128)} %prob.1), custom_call_target="tpu_custom_call" | custom-call | tf_op jit(solution)/shard_map/panel/pallas_call | solution.py:413
  111.0 1.9 %copy.10 = f32[512,256]{1,0:T(8,128)} copy(f32[512,256]{1,0:T(8,128)} %get-tuple-element.8) | data formatting | bytes 1048576
  112.9 1.4 %copy.11 = f32[1,32,256]{2,1,0:T(8,128)} copy(f32[1,32,256]{2,1,0:T(8,128)} %bitcast.6) | data formatting | bytes 65536

commit v3 on v2

v3 whole, which is shorter than its diff:
```python
import functools
import math

import jax
import jax.numpy as jnp
from jax import lax
from jax.experimental import pallas as pl
from jax.experimental.pallas import tpu as pltpu
from jax.sharding import PartitionSpec as P

N1 = 131072
MESH = pl.DeviceIdType.MESH
HIGHEST = lax.Precision.HIGHEST
F32 = jnp.float32
BF16 = jnp.bfloat16
I16 = jnp.int16
LANES = 128
CORES, XHI, XLO = 2, 2, 2
TOP = 32767.0
BASE, PANEL = 128, 16


def dot(a, b, ca, cb, precision=None):
    return lax.dot_general(
        a, b, (((ca,), (cb,)), ((), ())), precision=precision, preferred_element_type=F32
    )


def split(own, share):
    part = max(16, int(own * share / 16 + 0.5) * 16)
    return own - part, part


def encode(x, code, scale):
    peak = jnp.maximum(jnp.max(jnp.abs(x), axis=0, keepdims=True), 1e-30)
    code[...] = jnp.round(x * (TOP / peak)).astype(jnp.int32).astype(I16)
    scale[...] = peak * (1.0 / TOP)


def decode(code, scale):
    return code.astype(jnp.int32).astype(F32) * scale


def eliminate(work, inv, hooks):
    size = work.shape[0]
    shape = (PANEL, size)
    row = lax.broadcasted_iota(jnp.int32, shape, 0)
    spread = lambda x: jnp.broadcast_to(x, shape)
    left, right = slice(0, size), slice(size, 2 * size)
    for at in range(0, size, PANEL):
        here = slice(at, at + PANEL)
        block, side = work[here, left], work[here, right]
        cs = [spread(block[:, at + j : at + j + 1]) for j in range(PANEL)]
        pivots = jnp.zeros(shape, F32)
        for j in range(PANEL):
            pivots = jnp.where(row == j, cs[j], pivots)
            m = jnp.where(row > j, cs[j] * spread(1.0 / cs[j][j : j + 1, :]), 0.0)
            for k in range(j + 1, PANEL):
                cs[k] = cs[k] - m * spread(cs[k][j : j + 1, :])
            block = block - m * spread(block[j : j + 1, :])
            side = side - m * spread(side[j : j + 1, :])
        r = lax.rsqrt(pivots)
        r = r * (1.5 - 0.5 * pivots * r * r)
        block, side = block * r, side * r
        inv[here, :] = side
        turned = jnp.transpose(block)
        for to in range(at + PANEL, size, PANEL):
            there = slice(to, to + PANEL)
            a, b = work[there, left], work[there, right]
            for j in range(PANEL):
                t = spread(turned[there, j : j + 1])
                a = a - t * spread(block[j : j + 1, :])
                b = b - t * spread(side[j : j + 1, :])
            work[there, left] = a
            work[there, right] = b
        hooks.pop(0)()


def inverse_factor(a, work, inv, hooks):
    n = a.shape[0]
    if n == BASE:
        i = lax.broadcasted_iota(jnp.int32, (n, n), 0)
        j = lax.broadcasted_iota(jnp.int32, (n, n), 1)
        work[...] = jnp.concatenate([a, (i == j).astype(F32)], axis=1)
        eliminate(work, inv, hooks)
        return inv[...]
    h = n // 2
    w11 = inverse_factor(a[:h, :h], work, inv, hooks)
    l21 = dot(a[h:, :h], w11, 1, 1, HIGHEST)
    w22 = inverse_factor(a[h:, h:] - dot(l21, l21, 1, 1, HIGHEST), work, inv, hooks)
    w21 = -dot(dot(w22, l21, 1, 0, HIGHEST), w11, 1, 0, HIGHEST)
    top = jnp.concatenate([w11, jnp.zeros((h, h), F32)], axis=1)
    return jnp.concatenate([top, jnp.concatenate([w21, w22], axis=1)], axis=0)


class Mail:
    def __init__(self, send, recv):
        self.send, self.recv, self.ids, self.started = send, recv, {}, {}

    def copy(self, key, src, dst, where):
        k = self.ids.setdefault(key, len(self.ids))
        return pltpu.make_async_remote_copy(
            src_ref=src, dst_ref=dst, send_sem=self.send.at[k], recv_sem=self.recv.at[k],
            device_id=where, device_id_type=MESH,
        )

    def start(self, key, src, dst, where, whole=None):
        self.copy(key, src() if callable(src) else src, dst, where).start()
        assert whole is not None or key not in self.started, key
        self.started[key] = (src if whole is None else whole, where)

    def take(self, key, dst, where):
        self.copy(key, dst, dst, where).wait_recv()

    def close(self):
        for key, (ref, where) in self.started.items():
            ref = ref() if callable(ref) else ref
            self.copy(key, ref, ref, where).wait_send()


def kernel(
    groups, count, border, inverse, prior_hbm, sel, asg, prob, panel, out,
    big, minv, prior, flat, rows, got1, got2, q0, qh, qx, qz, qv, qg, q, picked, project,
    corner, corner_got, corner_sum, ya, ya_s, ya_g, ya_sg, xb, xb_s, xb_g, xb_sg,
    xa, xa_s, xa_g, xa_sg, yb, yb_s, yb_g, yb_sg, keep0, keep_a, keep_b, hit, work, invb,
    pan, acc, sums, core_got, keep1, z_code, z_scale, z_got, z_sgot,
    load, send, recv,
):
    grp, dev = lax.axis_index("grp"), lax.axis_index("dev")
    depth = count // (CORES * XHI)
    z, xhi, core = dev // (CORES * XHI), (dev // CORES) % XHI, dev % CORES
    at = lambda zz, xx, cc: (grp, (zz * XHI + xx) * CORES + cc)
    cpart, xpart = at(z, xhi, 1 - core), at(z, 1 - xhi, core)
    zparts = {o: at((z + o) % depth, xhi, core) for o in range(1, depth)}
    far = sorted(range(depth), key=lambda o: -min(o, depth - o))
    chips = [(o, x) for o in far for x in (1, 0) if (o, x) != (0, 0)]
    chip = {c: at((z + c[0]) % depth, xhi ^ c[1], core) for c in chips}
    slot = {c: i for i, c in enumerate(chips)}
    ys = [y for y in (2, 1, 3) if y < groups // XLO]
    near = [o for o in (5, 4, 7, 6, 3, 2, 1) if o < groups]
    peer = {o: (grp ^ o, dev) for o in near}
    width, size = picked.shape
    own = prior.shape[0]
    mail = Mail(send, recv)

    def fenced(f, *args):
        pl.when(grp >= 0)(functools.partial(f, *args))

    loads = {o: pltpu.make_async_copy(border.at[pl.ds((grp ^ o) * own, own)], big.at[o], load.at[o]) for o in range(groups)}
    loads["prior"] = pltpu.make_async_copy(prior_hbm, prior, load.at[groups])
    loads["inverse"] = pltpu.make_async_copy(inverse, minv, load.at[groups + 1])
    for name in ["prior"] + list(range(groups)) + ["inverse"]:
        loads[name].start()
    barrier = pltpu.get_barrier_semaphore()
    partners = [cpart] + list(chip.values()) + list(peer.values())
    for where in partners:
        pl.semaphore_signal(barrier, inc=1, device_id=where, device_id_type=MESH)

    want = jnp.transpose(jnp.broadcast_to(sel[...], (LANES, width)))[:, :1]
    want = jnp.broadcast_to(want, (width, own))
    lanes = lax.broadcasted_iota(jnp.int32, (width, own), 1)
    first = (dev * groups + grp) * own
    loads["prior"].wait()
    mine = dot((want - first == lanes).astype(F32).astype(BF16), prior[...], 1, 0).astype(BF16)
    for c in range(2):
        q0[pl.ds(c * width, width), :] = mine[:, c * LANES : (c + 1) * LANES]
    total = None
    for o in range(groups):
        loads[o].wait()
        base = (dev * groups + (grp ^ o)) * own
        part = dot((want - base == lanes).astype(F32).astype(BF16), big[o], 1, 0)
        total = part if total is None else total + part
    total = total.astype(BF16)
    for c in range(size // LANES):
        flat[pl.ds(c * width, width), :] = total[:, c * LANES : (c + 1) * LANES]
    pl.semaphore_wait(barrier, len(partners))

    high = flat.shape[0]
    half, quarter, bit = high // CORES, high // (CORES * XHI), high // count
    qhalf, qquart, qbit = 2 * width // CORES, 2 * width // (CORES * XHI), 2 * width // count
    at1 = core * half
    at3 = at1 + xhi * quarter + z * bit
    qat1 = core * qhalf
    qat2 = qat1 + xhi * qquart
    qat3 = qat2 + z * qbit
    mail.start("r1", flat.at[pl.ds((1 - core) * half, half)], got1, cpart)
    mail.start("q1", q0.at[pl.ds((1 - core) * qhalf, qhalf)], qh, cpart)
    mail.take("r1", got1, cpart)
    flat[pl.ds(at1, half), :] = flat[pl.ds(at1, half), :] + got1[...]
    for c in chips:
        there = at1 + (xhi ^ c[1]) * quarter + ((z + c[0]) % depth) * bit
        mail.start("r2", flat.at[pl.ds(there, bit)], got2.at[slot[c]], chip[c], got2)
    mail.take("q1", qh, cpart)
    q0[pl.ds(qat1, qhalf), :] = q0[pl.ds(qat1, qhalf), :] + qh[...]
    mail.start("q2", q0.at[pl.ds(qat1 + (1 - xhi) * qquart, qquart)], qx, xpart)
    ids = first + lax.broadcasted_iota(jnp.int32, (own, width), 0)
    marked = jnp.max((ids == sel[...]).astype(F32), axis=1, keepdims=True)
    hit[...] = jnp.broadcast_to(marked, hit.shape)
    mail.take("q2", qx, xpart)
    q0[pl.ds(qat2, qquart), :] = q0[pl.ds(qat2, qquart), :] + qx[...]
    for o in zparts:
        mail.start("q3", q0.at[pl.ds(qat2 + ((z + o) % depth) * qbit, qbit)], qz.at[o - 1], zparts[o], qz)
    mail.take("r2", got2, xpart)
    value = flat[pl.ds(at3, bit), :]
    for c in chips:
        value = value + got2[slot[c]]
    rows[pl.ds(at3, bit), :] = value
    here = rows.at[pl.ds(at3, bit)]
    rings = [chips[i : i + 5] for i in range(0, len(chips), 5)]
    for n, ring in enumerate(rings):
        for c in ring:
            mail.start(("r3", n), here, here, chip[c], got2.at[pl.ds(0, len(ring))])
    other = rows.at[pl.ds((1 - core) * half, half)]
    mail.start("r4", here, here, cpart, other)
    value = q0[pl.ds(qat3, qbit), :]
    if zparts:
        mail.take("q3", qz, xpart)
    for o in zparts:
        value = value + qz[o - 1]
    qv[...] = value
    for n, o in enumerate(near):
        mail.start("q4", qv, qg.at[n], peer[o], qg)

    def forward(n):
        mail.take(("r3", n), got2.at[pl.ds(0, len(rings[n]))], xpart)
        for c in rings[n]:
            there = rows.at[pl.ds(at1 + (xhi ^ c[1]) * quarter + ((z + depth - c[0]) % depth) * bit, bit)]
            mail.start("r4", there, there, cpart, other)

    order = list(range(len(rings)))[::-1]
    forward(order[0])
    mail.take("q4", qg, xpart)
    value = qv[...]
    for n in range(len(near)):
        value = value + qg[n]
    q[pl.ds(qat3, qbit), :] = value
    here = q.at[pl.ds(qat3, qbit)]
    mail.start("q5", here, here, xpart)
    for n in order[1:]:
        forward(n)
    mail.take("r4", other, cpart)

    for c in range(size // LANES):
        picked[:, c * LANES : (c + 1) * LANES] = rows[pl.ds(c * width, width), :]
    loads["inverse"].wait()
    project[...] = dot(minv[...], picked[...], 1, 1).astype(BF16)
    scenario = asg[grp]
    weight = 0.0
    for i in range(groups):
        weight = weight + jnp.where(scenario == i, prob[i], 0.0)
    corner[...] = weight * dot(picked[...], project[...], 1, 0)
    chalf, cpiece = width // CORES, width // CORES // depth
    cmine = pl.ds(core * chalf + z * cpiece, cpiece)
    for n, o in enumerate(near):
        mail.start("c1", corner.at[cmine], corner_got.at[n], peer[o], corner_got)
    ra, rb = split(own, 0.5)

    def block(o):
        return weight * jnp.dot(big[o], project[...], preferred_element_type=F32)

    def make(y):
        side = block(2 * y + 1)
        encode(side[ra:], xb.at[y], xb_s.at[y])
        if y:
            encode(side[:ra], ya.at[y, 1], ya_s.at[y, 1])
            same = block(2 * y)
            encode(same[:ra], ya.at[y, 0], ya_s.at[y, 0])
            keep_b[y] = same[ra:]
        else:
            keep_a[...] = side[:ra]

    def ship(y):
        mail.start(("xbs", y), lambda: xb_s.at[y], xb_sg.at[y], peer[1])
        mail.start(("xb", y), lambda: xb.at[y], xb_g.at[y], peer[1])
        if y:
            mail.start(("yas", y), lambda: ya_s.at[y], ya_sg.at[y], peer[2 * y])
            mail.start(("ya", y), lambda: ya.at[y], ya_g.at[y], peer[2 * y])

    lots = q.at[pl.ds(0, XHI * (depth - 1) * qbit)]
    rest = corner_sum.at[pl.ds(0, (depth - 1) * cpiece)]

    def blocks(y):
        make(y)
        ship(y)

    def corner_out():
        mail.take("c1", corner_got, xpart)
        value = corner[cmine, :]
        for n in range(len(near)):
            value = value + corner_got[n]
        corner_sum[cmine, :] = value
        here = corner_sum.at[cmine]
        for o in zparts:
            mail.start("c2", here, here, zparts[o], lambda: rest)

    def prior_out():
        mail.take("q5", q.at[pl.ds(qat1 + (1 - xhi) * qquart + z * qbit, qbit)], xpart)
        for o in zparts:
            for x in range(XHI):
                here = q.at[pl.ds(qat1 + x * qquart + z * qbit, qbit)]
                mail.start("q6", here, here, zparts[o], lambda: lots)

    def prior_over():
        if zparts:
            mail.take("q6", lots, xpart)
        here = lambda: q.at[pl.ds(qat1, qhalf)]
        mail.start("q7", here, here(), cpart)

    for y in ys[:1]:
        fenced(blocks, y)
    fenced(prior_out)
    for y in ys[1:2]:
        fenced(blocks, y)
    fenced(corner_out)
    for y in ys[2:] + [0]:
        fenced(blocks, y)
    fenced(prior_over)
    keep0[...] = block(0)
    mail.take("q7", q.at[pl.ds((1 - core) * qhalf, qhalf)], cpart)
    picks = jnp.concatenate([q[pl.ds(c * width, width), :] for c in range(2)], axis=1)
    keep0[...] -= dot(prior[...], picks, 1, 1)
    less = dot(picks, picks, 1, 1)
    if zparts:
        mail.take("c2", rest, xpart)
    here = corner_sum.at[pl.ds(core * chalf, chalf)]
    mail.start("c3", here, here, cpart)
    mail.take("c3", corner_sum.at[pl.ds((1 - core) * chalf, chalf)], cpart)
    a = corner_sum[...] - less
    a = 0.5 * (a + jnp.transpose(a))

    def onward(y):
        mail.take(("xbs", y), xb_sg.at[y], peer[1])
        mail.take(("xb", y), xb_g.at[y], peer[1])
        encode(keep_b[y] + decode(xb_g[y], xb_sg[y]), yb.at[y], yb_s.at[y])
        mail.start(("ybs", y), lambda: yb_s.at[y], yb_sg.at[y], peer[2 * y])
        mail.start(("yb", y), lambda: yb.at[y], yb_g.at[y], peer[2 * y])

    def across():
        value, here = keep_a[...], keep0[:ra, :]
        for y in ys:
            mail.take(("yas", y), ya_sg.at[y], peer[2 * y])
            mail.take(("ya", y), ya_g.at[y], peer[2 * y])
            value = value + decode(ya_g[y, 1], ya_sg[y, 1])
            here = here + decode(ya_g[y, 0], ya_sg[y, 0])
        encode(value, xa, xa_s)
        mail.start("xas", xa_s, xa_sg, peer[1])
        mail.start("xa", xa, xa_g, peer[1])
        keep0[:ra, :] = here

    hooks = [lambda: None for _ in range(width // PANEL)]
    for y, n in zip(ys, (0, 1, 4)):
        hooks[n] = functools.partial(fenced, onward, y)
    hooks[7] = functools.partial(fenced, across)
    w = inverse_factor(a, work, invb, hooks)

    mail.take("xas", xa_sg, peer[1])
    mail.take("xa", xa_g, peer[1])
    mail.take(("xbs", 0), xb_sg.at[0], peer[1])
    mail.take(("xb", 0), xb_g.at[0], peer[1])
    upper = keep0[:ra, :] + decode(xa_g[...], xa_sg[...])
    lower = keep0[ra:, :] + decode(xb_g[0], xb_sg[0])
    for y in ys:
        mail.take(("ybs", y), yb_sg.at[y], peer[2 * y])
        mail.take(("yb", y), yb_g.at[y], peer[2 * y])
        lower = lower + decode(yb_g[y], yb_sg[y])
    solved = dot(jnp.concatenate([upper, lower], axis=0), w, 1, 1, HIGHEST)
    solved = jnp.where(hit[...] > 0.5, 0.0, solved)
    panel[...] = solved
    pan[0] = solved.astype(BF16)

    pa, pb = split(own, 0.4)
    top, low = pl.ds(0, pa), pl.ds(pa, pb)
    mail.start("g1", pan.at[0, low], pan.at[1, low], peer[1])
    for y in ys:
        mail.start(("g2", y), pan.at[0, top], pan.at[2 * y, top], peer[2 * y])
    mail.start("g3", pan.at[0, top], pan.at[1, top], peer[1])
    for y in ys:
        mail.start(("g4", y), pan.at[0, low], pan.at[2 * y, low], peer[2 * y])
    acc[...] = dot(pan[0], big[0], 0, 0)
    mail.take("g1", pan.at[1, low], peer[1])
    for y in ys:
        mail.start(("g5", y), pan.at[1, low], pan.at[2 * y + 1, low], peer[2 * y])
    for y in ys[1:] + ys[:1]:
        mail.take(("g2", y), pan.at[2 * y, top], peer[2 * y])
        mail.start(("g6", y), pan.at[2 * y, top], pan.at[2 * y + 1, top], peer[1])
    mail.take("g3", pan.at[1, top], peer[1])
    acc[...] += dot(pan[1], big[1], 0, 0)
    for y in ys[1:] + ys[:1]:
        mail.take(("g4", y), pan.at[2 * y, low], peer[2 * y])
        acc[...] += dot(pan[2 * y], big[2 * y], 0, 0)
    for y in ys[1:] + ys[:1]:
        mail.take(("g5", y), pan.at[2 * y + 1, low], peer[2 * y])
        mail.take(("g6", y), pan.at[2 * y + 1, top], peer[1])
        acc[...] += dot(pan[2 * y + 1], big[2 * y + 1], 0, 0)

    piece = sums.shape[3]
    scale = 1.0 / math.sqrt(N1)
    halves = [range(0, (depth + 1) // 2), range((depth + 1) // 2, depth)]
    halves = [h for h in halves if len(h)]
    tiles = acc.shape[1] // LANES
    done = 0
    for e in range(tiles):
        turned = jnp.transpose(acc[:, e * LANES : (e + 1) * LANES]) * scale
        for k in range(LANES // piece):
            n = e * (LANES // piece) + k
            zz, xx, cc = n // (XHI * CORES), (n // CORES) % XHI, n % CORES
            sums[cc, zz, xx] = turned[k * piece : (k + 1) * piece, :]
        if done < len(halves) and n + 1 == len(halves[done]) * XHI * CORES + (halves[done][0]) * XHI * CORES:
            part = pl.ds(halves[done][0], len(halves[done]))
            mail.start(("s1", done), sums.at[1 - core, part], core_got.at[part], cpart)
            done += 1
    assert done == len(halves)
    for n, h in enumerate(halves):
        mail.take(("s1", n), core_got.at[pl.ds(h[0], len(h))], cpart)
    value = (sums[core] + core_got[...]).reshape(depth * XHI * piece, width)
    keep1[...] = value.reshape(keep1.shape)
    peak = jnp.maximum(jnp.max(jnp.abs(value), axis=0, keepdims=True), 1e-30)
    z_scale[...] = peak * (1.0 / TOP)
    z_code[...] = jnp.round(value * (TOP / peak)).astype(jnp.int32).astype(I16).reshape(z_code.shape)
    for c in chips:
        mail.start("s2s", z_scale, z_sgot.at[slot[c]], chip[c], z_sgot)
        mail.start("s2", z_code.at[(z + c[0]) % depth, xhi ^ c[1]], z_got.at[slot[c]], chip[c], z_got)
    mail.take("s2s", z_sgot, xpart)
    mail.take("s2", z_got, xpart)
    value = keep1[z, xhi]
    for n in range(len(chips)):
        value = value + decode(z_got[n], z_sgot[n])
    out[...] = value
    mail.close()
    assert len(mail.ids) <= send.shape[0], len(mail.ids)


def call(groups, count, border, inverse, prior, sel, asg, prob):
    size = border.shape[1]
    own, width = prior.shape
    depth = count // (CORES * XHI)
    messages = 56
    n = max(depth - 1, 1)
    others = depth * XHI - 1
    piece = size // count
    high = size // LANES * width
    ny = groups // XLO
    ra, rb = split(own, 0.5)
    dma, vmem = pltpu.SemaphoreType.DMA, pltpu.VMEM
    vm = pl.BlockSpec(memory_space=vmem)
    anyspace = pl.BlockSpec(memory_space=pl.ANY)
    sm = pl.BlockSpec(memory_space=pltpu.SMEM)
    return pl.pallas_call(
        functools.partial(kernel, groups, count),
        out_shape=(jax.ShapeDtypeStruct((own, width), F32), jax.ShapeDtypeStruct((piece, width), F32)),
        in_specs=[anyspace, anyspace, anyspace, vm, sm, sm],
        out_specs=(vm, vm),
        scratch_shapes=[
            vmem((groups, own, size), BF16),
            vmem((size, size), BF16),
            vmem((own, width), BF16),
            vmem((high, LANES), BF16),
            vmem((high, LANES), BF16),
            vmem((high // CORES, LANES), BF16),
            vmem((others, high // count, LANES), BF16),
            vmem((2 * width, LANES), BF16),
            vmem((2 * width // CORES, LANES), BF16),
            vmem((2 * width // (CORES * XHI), LANES), BF16),
            vmem((n, 2 * width // count, LANES), BF16),
            vmem((2 * width // count, LANES), BF16),
            vmem((groups - 1, 2 * width // count, LANES), BF16),
            vmem((2 * width, LANES), BF16),
            vmem((width, size), BF16),
            vmem((size, width), BF16),
            vmem((width, width), F32),
            vmem((groups - 1, width // CORES // depth, width), F32),
            vmem((width, width), F32),
            vmem((ny, 2, ra, width), I16),
            vmem((ny, 2, 1, width), F32),
            vmem((ny, 2, ra, width), I16),
            vmem((ny, 2, 1, width), F32),
            vmem((ny, rb, width), I16),
            vmem((ny, 1, width), F32),
            vmem((ny, rb, width), I16),
            vmem((ny, 1, width), F32),
            vmem((ra, width), I16),
            vmem((1, width), F32),
            vmem((ra, width), I16),
            vmem((1, width), F32),
            vmem((ny, rb, width), I16),
            vmem((ny, 1, width), F32),
            vmem((ny, rb, width), I16),
            vmem((ny, 1, width), F32),
            vmem((own, width), F32),
            vmem((ra, width), F32),
            vmem((ny, rb, width), F32),
            vmem((own, width), F32),
            vmem((BASE, 2 * BASE), F32),
            vmem((BASE, BASE), F32),
            vmem((groups, own, width), BF16),
            vmem((width, size), F32),
            vmem((CORES, depth, XHI, piece, width), F32),
            vmem((depth, XHI, piece, width), F32),
            vmem((depth, XHI, piece, width), F32),
            vmem((depth, XHI, piece, width), I16),
            vmem((1, width), F32),
            vmem((others, piece, width), I16),
            vmem((others, 1, width), F32),
            dma((groups + 2,)),
            dma((messages,)),
            dma((messages,)),
        ],
        compiler_params=pltpu.CompilerParams(
            collective_id=0, has_side_effects=True, vmem_limit_bytes=60 << 20
        ),
        name="panel",
    )(border, inverse, prior, sel, asg, prob)


def body(border, inverse_blocks, selected, assignment, probability, prior_panel):
    groups, count = lax.axis_size("grp"), lax.axis_size("dev")
    panel, residual = call(
        groups, count, border[0], inverse_blocks[0], prior_panel, selected[None, :], assignment, probability
    )
    return (panel, residual[None])


def solution(mesh):
    return jax.shard_map(
        body,
        mesh=mesh,
        in_specs=(
            P("grp", "dev", None),
            P("grp", None, None),
            P(),
            P(),
            P(),
            P(("dev", "grp"), None),
        ),
        out_specs=(P(("dev", "grp"), None), P("grp", "dev", None)),
        check_vma=False,
    )
```

time: 115 us -> 94.6 us (0.82)
  Pallas kernels: 110 us -> 90.5 us
    pallas_call x1, Pallas kernels: 110 us -> 90.5 us  [call(): pl.pallas_call(functools.partial(kernel, groups, count), out_shape=(jax.S...]
where the time goes in v3:
time: 94.6 us; the launch traced here: 94.4 us
  Pallas kernels  90.5 us (96%)
  local copies, waits for them, and re-layouts  3.24 us (3%)
    pallas_call x1, Pallas kernels, call(): pl.pallas_call(functools.partial(kernel, groups, count), out_shape=(jax.S...  90.5 us
    unnamed x2, local copies, waits for them, and re-layouts  3.24 us

profile of v3, /device:TPU:1, one launch (start us, length us, event | category | flops | bytes accessed | tf_op | source)
XLA Modules:
  0.0 94.4 jit_solution(4202372455858702378)
XLA Ops:
  0.6 90.5 %panel.1 = (f32[512,256]{1,0:T(8,128)}, f32[32,256]{1,0:T(8,128)}) custom-call(bf16[4096,1024]{1,0:T(8,128)(2,1)} %bitcast.4, bf16[1024,1024]{1,0:T(8,128)(2,1)} %bitcast.5, bf16[512,256]{1,0:T(8,128)(2,1)} %prior_hbm.1, s32[1,256]{1,0:T(1,128)} %bitcast.7, s32[8]{0:T(128)} %asg.1, f32[8]{0:T(128)} %prob.1), custom_call_target="tpu_custom_call" | custom-call | tf_op jit(solution)/shard_map/panel/pallas_call | solution.py:448
  91.1 1.9 %copy.10 = f32[512,256]{1,0:T(8,128)} copy(f32[512,256]{1,0:T(8,128)} %get-tuple-element.8) | data formatting | bytes 1048576
  93.0 1.4 %copy.11 = f32[1,32,256]{2,1,0:T(8,128)} copy(f32[1,32,256]{2,1,0:T(8,128)} %bitcast.6) | data formatting | bytes 65536

commit v4 on v3

--- a/solution.py
+++ b/solution.py
@@ -64,8 +64,8 @@
         block, side = block * r, side * r
         inv[here, :] = side
         turned = jnp.transpose(block)
-        for to in range(at + PANEL, size, PANEL):
-            there = slice(to, to + PANEL)
+        if at + PANEL < size:
+            there = slice(at + PANEL, at + 2 * PANEL)
             a, b = work[there, left], work[there, right]
             for j in range(PANEL):
                 t = spread(turned[there, j : j + 1])
@@ -73,6 +73,10 @@
                 b = b - t * spread(side[j : j + 1, :])
             work[there, left] = a
             work[there, right] = b
+        if at + 2 * PANEL < size:
+            there = slice(at + 2 * PANEL, size)
+            update = dot(block, jnp.concatenate([block, side], axis=1), 0, 0, HIGHEST)
+            work[there, :] = work[there, :] - update[there, :]
         hooks.pop(0)()
 
 
@@ -122,7 +126,7 @@
     groups, count, border, inverse, prior_hbm, sel, asg, prob, panel, out,
     big, minv, prior, flat, rows, got1, got2, q0, qh, qx, qz, qv, qg, q, picked, project,
     corner, corner_got, corner_sum, ya, ya_s, ya_g, ya_sg, xb, xb_s, xb_g, xb_sg,
-    xa, xa_s, xa_g, xa_sg, yb, yb_s, yb_g, yb_sg, keep0, keep_a, keep_b, hit, work, invb,
+    xa, xa_s, xa_g, xa_sg, yb, yb_s, yb_g, yb_sg, keep0, solution_rows, keep_a, keep_b, hit, work, invb,
     pan, acc, sums, core_got, keep1, z_code, z_scale, z_got, z_sgot,
     load, send, recv,
 ):
@@ -248,12 +252,14 @@
     weight = 0.0
     for i in range(groups):
         weight = weight + jnp.where(scenario == i, prob[i], 0.0)
-    corner[...] = weight * dot(picked[...], project[...], 1, 0)
-    chalf, cpiece = width // CORES, width // CORES // depth
-    cmine = pl.ds(core * chalf + z * cpiece, cpiece)
+    turn = min(4, depth)
+    steps = {4: (2, 1, depth - 1), 2: (1,), 1: ()}[turn]
+    chalf, cpiece = width // CORES, width // CORES // turn
+    cmine = pl.ds(core * chalf + z % turn * cpiece, cpiece)
+    corner[...] = weight * dot(picked[cmine, :], project[...], 1, 0)
     for n, o in enumerate(near):
-        mail.start("c1", corner.at[cmine], corner_got.at[n], peer[o], corner_got)
-    ra, rb = split(own, 0.5)
+        mail.start("c1", corner, corner_got.at[n], peer[o], corner_got)
+    ra, rb = split(own, 0.56)
 
     def block(o):
         return weight * jnp.dot(big[o], project[...], preferred_element_type=F32)
@@ -277,7 +283,7 @@
             mail.start(("ya", y), lambda: ya.at[y], ya_g.at[y], peer[2 * y])
 
     lots = q.at[pl.ds(0, XHI * (depth - 1) * qbit)]
-    rest = corner_sum.at[pl.ds(0, (depth - 1) * cpiece)]
+    rest = corner_sum.at[pl.ds(0, (turn - 1) * cpiece)]
 
     def blocks(y):
         make(y)
@@ -285,12 +291,12 @@
 
     def corner_out():
         mail.take("c1", corner_got, xpart)
-        value = corner[cmine, :]
+        value = corner[...]
         for n in range(len(near)):
             value = value + corner_got[n]
         corner_sum[cmine, :] = value
         here = corner_sum.at[cmine]
-        for o in zparts:
+        for o in steps:
             mail.start("c2", here, here, zparts[o], lambda: rest)
 
     def prior_out():
@@ -347,51 +353,91 @@
         mail.start("xa", xa, xa_g, peer[1])
         keep0[:ra, :] = here
 
+    def gather():
+        mail.take("xas", xa_sg, peer[1])
+        mail.take("xa", xa_g, peer[1])
+        mail.take(("xbs", 0), xb_sg.at[0], peer[1])
+        mail.take(("xb", 0), xb_g.at[0], peer[1])
+        keep0[:ra, :] = keep0[:ra, :] + decode(xa_g[...], xa_sg[...])
+        lower = keep0[ra:, :] + decode(xb_g[0], xb_sg[0])
+        for y in ys:
+            mail.take(("ybs", y), yb_sg.at[y], peer[2 * y])
+            mail.take(("yb", y), yb_g.at[y], peer[2 * y])
+            lower = lower + decode(yb_g[y], yb_sg[y])
+        keep0[ra:, :] = lower
+
     hooks = [lambda: None for _ in range(width // PANEL)]
     for y, n in zip(ys, (0, 1, 4)):
         hooks[n] = functools.partial(fenced, onward, y)
     hooks[7] = functools.partial(fenced, across)
+    hooks[15] = functools.partial(fenced, gather)
     w = inverse_factor(a, work, invb, hooks)
 
-    mail.take("xas", xa_sg, peer[1])
-    mail.take("xa", xa_g, peer[1])
-    mail.take(("xbs", 0), xb_sg.at[0], peer[1])
-    mail.take(("xb", 0), xb_g.at[0], peer[1])
-    upper = keep0[:ra, :] + decode(xa_g[...], xa_sg[...])
-    lower = keep0[ra:, :] + decode(xb_g[0], xb_sg[0])
-    for y in ys:
-        mail.take(("ybs", y), yb_sg.at[y], peer[2 * y])
-        mail.take(("yb", y), yb_g.at[y], peer[2 * y])
-        lower = lower + decode(yb_g[y], yb_sg[y])
-    solved = dot(jnp.concatenate([upper, lower], axis=0), w, 1, 1, HIGHEST)
-    solved = jnp.where(hit[...] > 0.5, 0.0, solved)
-    panel[...] = solved
-    pan[0] = solved.astype(BF16)
-
-    pa, pb = split(own, 0.4)
+    pa, pb = split(own, 0.53)
     top, low = pl.ds(0, pa), pl.ds(pa, pb)
+
+    def solve(rows):
+        solved = dot(keep0[rows, :], w, 1, 1, HIGHEST)
+        solved = jnp.where(hit[rows, :] > 0.5, 0.0, solved)
+        solution_rows[rows, :] = solved
+        pan[0, rows, :] = solved.astype(BF16)
+
+    tops = [pl.ds(0, pa // 32 * 16), pl.ds(pa // 32 * 16, pa - pa // 32 * 16)]
+    lows = [pl.ds(pa, pb // 32 * 16), pl.ds(pa + pb // 32 * 16, pb - pb // 32 * 16)]
+    ends = [y for y in (1, 3) if y < groups // XLO]
+    relay = 2 in ys
+
+    def add(o):
+        acc[...] += dot(pan[o], big[o], 0, 0)
+
+    def pass_on(kind, y, x, pieces, n):
+        if relay:
+            mail.start((kind, n), pan.at[2 * y + x, pieces[n]], pan.at[4 + x, pieces[n]], peer[2 * (y ^ 2)])
+
+    def passed(kind, x, pieces):
+        for n in range(2):
+            mail.take((kind, n), pan.at[4 + x, pieces[n]], peer[2 * ends[1 - n]])
+
+    solve(slice(0, pa))
+    for y in ends:
+        mail.start(("g2", y), pan.at[0, top], pan.at[2 * y, top], peer[2 * y])
+    solve(slice(pa, own))
     mail.start("g1", pan.at[0, low], pan.at[1, low], peer[1])
-    for y in ys:
-        mail.start(("g2", y), pan.at[0, top], pan.at[2 * y, top], peer[2 * y])
     mail.start("g3", pan.at[0, top], pan.at[1, top], peer[1])
-    for y in ys:
+    for y in ends:
         mail.start(("g4", y), pan.at[0, low], pan.at[2 * y, low], peer[2 * y])
+    written = pltpu.make_async_copy(solution_rows, panel, load.at[groups])
+    written.start()
     acc[...] = dot(pan[0], big[0], 0, 0)
+    for n, y in enumerate(ends):
+        mail.take(("g2", y), pan.at[2 * y, top], peer[2 * y])
+        pass_on("h2", y, 0, tops, n)
+        mail.start(("g6", y), pan.at[2 * y, top], pan.at[2 * y + 1, top], peer[1])
     mail.take("g1", pan.at[1, low], peer[1])
-    for y in ys:
+    for y in ends:
         mail.start(("g5", y), pan.at[1, low], pan.at[2 * y + 1, low], peer[2 * y])
-    for y in ys[1:] + ys[:1]:
-        mail.take(("g2", y), pan.at[2 * y, top], peer[2 * y])
-        mail.start(("g6", y), pan.at[2 * y, top], pan.at[2 * y + 1, top], peer[1])
+    for n, y in enumerate(ends):
+        mail.take(("g4", y), pan.at[2 * y, low], peer[2 * y])
+        pass_on("h4", y, 0, lows, n)
     mail.take("g3", pan.at[1, top], peer[1])
-    acc[...] += dot(pan[1], big[1], 0, 0)
-    for y in ys[1:] + ys[:1]:
-        mail.take(("g4", y), pan.at[2 * y, low], peer[2 * y])
-        acc[...] += dot(pan[2 * y], big[2 * y], 0, 0)
-    for y in ys[1:] + ys[:1]:
+    add(1)
+    if relay:
+        passed("h2", 0, tops)
+        mail.start(("g6", 2), pan.at[4, top], pan.at[5, top], peer[1])
+    for y in ends:
+        add(2 * y)
+    for n, y in enumerate(ends):
         mail.take(("g5", y), pan.at[2 * y + 1, low], peer[2 * y])
+        pass_on("h5", y, 1, lows, n)
+    for y in ends:
         mail.take(("g6", y), pan.at[2 * y + 1, top], peer[1])
-        acc[...] += dot(pan[2 * y + 1], big[2 * y + 1], 0, 0)
+        add(2 * y + 1)
+    if relay:
+        passed("h4", 0, lows)
+        add(4)
+        mail.take(("g6", 2), pan.at[5, top], peer[1])
+        passed("h5", 1, lows)
+        add(5)
 
     piece = sums.shape[3]
     scale = 1.0 / math.sqrt(N1)
@@ -426,6 +472,7 @@
     for n in range(len(chips)):
         value = value + decode(z_got[n], z_sgot[n])
     out[...] = value
+    written.wait()
     mail.close()
     assert len(mail.ids) <= send.shape[0], len(mail.ids)
 
@@ -434,13 +481,13 @@
     size = border.shape[1]
     own, width = prior.shape
     depth = count // (CORES * XHI)
-    messages = 56
+    messages = 59
     n = max(depth - 1, 1)
     others = depth * XHI - 1
     piece = size // count
     high = size // LANES * width
     ny = groups // XLO
-    ra, rb = split(own, 0.5)
+    ra, rb = split(own, 0.56)
     dma, vmem = pltpu.SemaphoreType.DMA, pltpu.VMEM
     vm = pl.BlockSpec(memory_space=vmem)
     anyspace = pl.BlockSpec(memory_space=pl.ANY)
@@ -449,7 +496,7 @@
         functools.partial(kernel, groups, count),
         out_shape=(jax.ShapeDtypeStruct((own, width), F32), jax.ShapeDtypeStruct((piece, width), F32)),
         in_specs=[anyspace, anyspace, anyspace, vm, sm, sm],
-        out_specs=(vm, vm),
+        out_specs=(anyspace, vm),
         scratch_shapes=[
             vmem((groups, own, size), BF16),
             vmem((size, size), BF16),
@@ -467,8 +514,8 @@
             vmem((2 * width, LANES), BF16),
             vmem((width, size), BF16),
             vmem((size, width), BF16),
-            vmem((width, width), F32),
-            vmem((groups - 1, width // CORES // depth, width), F32),
+            vmem((width // CORES // min(4, depth), width), F32),
+            vmem((groups - 1, width // CORES // min(4, depth), width), F32),
             vmem((width, width), F32),
             vmem((ny, 2, ra, width), I16),
             vmem((ny, 2, 1, width), F32),
@@ -486,6 +533,7 @@
             vmem((ny, 1, width), F32),
             vmem((ny, rb, width), I16),
             vmem((ny, 1, width), F32),
+            vmem((own, width), F32),
             vmem((own, width), F32),
             vmem((ra, width), F32),
             vmem((ny, rb, width), F32),
@@ -512,11 +560,28 @@
     )(border, inverse, prior, sel, asg, prob)
 
 
+def finish_kernel(panel, residual, panel_out, residual_out):
+    panel_out[...] = panel[...]
+    residual_out[...] = residual[...]
+
+
+def finish(panel, residual):
+    vm = pl.BlockSpec(memory_space=pltpu.VMEM)
+    return pl.pallas_call(
+        finish_kernel,
+        out_shape=(jax.ShapeDtypeStruct(panel.shape, F32), jax.ShapeDtypeStruct(residual.shape, F32)),
+        in_specs=[vm, vm],
+        out_specs=(vm, vm),
+        name="finish",
+    )(panel, residual)
+
+
 def body(border, inverse_blocks, selected, assignment, probability, prior_panel):
     groups, count = lax.axis_size("grp"), lax.axis_size("dev")
     panel, residual = call(
         groups, count, border[0], inverse_blocks[0], prior_panel, selected[None, :], assignment, probability
     )
+    panel, residual = finish(panel, residual)
     return (panel, residual[None])
 
 

time: 94.6 us -> 90.2 us (0.953)
  local copies, waits for them, and re-layouts: 3.24 us -> 0 us
  Pallas kernels: 90.5 us -> 89.4 us
    unnamed x2 -> x0, local copies, waits for them, and re-layouts: 3.24 us -> none
    pallas_call x1, Pallas kernels: 90.5 us -> 87.6 us  [call(): pl.pallas_call(functools.partial(kernel, groups, count), out_shape=(jax.S...]
    pallas_call x0 -> x1, Pallas kernels: none -> 1.87 us  [finish(): pl.pallas_call(finish_kernel, out_shape=(jax.ShapeDtypeStruct(panel.shape...]
where the time goes in v4:
time: 90.2 us; the launch traced here: 90.1 us
  Pallas kernels  89.4 us (99%)
    pallas_call x1, Pallas kernels, call(): pl.pallas_call(functools.partial(kernel, groups, count), out_shape=(jax.S...  87.6 us
    pallas_call x1, Pallas kernels, finish(): pl.pallas_call(finish_kernel, out_shape=(jax.ShapeDtypeStruct(panel.shape...  1.87 us

profile of v4, /device:TPU:1, one launch (start us, length us, event | category | flops | bytes accessed | tf_op | source)
XLA Modules:
  0.0 90.1 jit_solution(1914589825157005765)
XLA Ops:
  0.6 87.6 %panel.1 = (f32[512,256]{1,0:T(8,128)}, f32[32,256]{1,0:T(8,128)}) custom-call(bf16[4096,1024]{1,0:T(8,128)(2,1)} %bitcast.4, bf16[1024,1024]{1,0:T(8,128)(2,1)} %bitcast.5, bf16[512,256]{1,0:T(8,128)(2,1)} %prior_hbm.1, s32[1,256]{1,0:T(1,128)} %bitcast.6, s32[8]{0:T(128)} %asg.1, f32[8]{0:T(128)} %prob.1), custom_call_target="tpu_custom_call" | custom-call | tf_op jit(solution)/shard_map/panel/pallas_call | solution.py:495
  88.2 1.9 %finish.1 = (f32[512,256]{1,0:T(8,128)}, f32[32,256]{1,0:T(8,128)}) custom-call(f32[512,256]{1,0:T(8,128)} %get-tuple-element.6.panel, f32[32,256]{1,0:T(8,128)} %get-tuple-element.7.residual), custom_call_target="tpu_custom_call" | custom-call | tf_op jit(solution)/shard_map/finish/pallas_call | solution.py:570

commit v5 on v4

--- a/solution.py
+++ b/solution.py
@@ -80,21 +80,13 @@
         hooks.pop(0)()
 
 
-def inverse_factor(a, work, inv, hooks):
+def eliminated(a, work, inv, hooks):
     n = a.shape[0]
-    if n == BASE:
-        i = lax.broadcasted_iota(jnp.int32, (n, n), 0)
-        j = lax.broadcasted_iota(jnp.int32, (n, n), 1)
-        work[...] = jnp.concatenate([a, (i == j).astype(F32)], axis=1)
-        eliminate(work, inv, hooks)
-        return inv[...]
-    h = n // 2
-    w11 = inverse_factor(a[:h, :h], work, inv, hooks)
-    l21 = dot(a[h:, :h], w11, 1, 1, HIGHEST)
-    w22 = inverse_factor(a[h:, h:] - dot(l21, l21, 1, 1, HIGHEST), work, inv, hooks)
-    w21 = -dot(dot(w22, l21, 1, 0, HIGHEST), w11, 1, 0, HIGHEST)
-    top = jnp.concatenate([w11, jnp.zeros((h, h), F32)], axis=1)
-    return jnp.concatenate([top, jnp.concatenate([w21, w22], axis=1)], axis=0)
+    i = lax.broadcasted_iota(jnp.int32, (n, n), 0)
+    j = lax.broadcasted_iota(jnp.int32, (n, n), 1)
+    work[...] = jnp.concatenate([a, (i == j).astype(F32)], axis=1)
+    eliminate(work, inv, hooks)
+    return inv[...]
 
 
 class Mail:
@@ -123,10 +115,10 @@
 
 
 def kernel(
-    groups, count, border, inverse, prior_hbm, sel, asg, prob, panel, out,
-    big, minv, prior, flat, rows, got1, got2, q0, qh, qx, qz, qv, qg, q, picked, project,
+    groups, count, border, inverse, prior_hbm, sel_hbm, asg_hbm, prob_hbm, panel, out,
+    sel, asg, prob, last, big, minv, prior, flat, rows, hot, got1, got2, q0, qh, qx, qz, qv, qg, q, picked, project,
     corner, corner_got, corner_sum, ya, ya_s, ya_g, ya_sg, xb, xb_s, xb_g, xb_sg,
-    xa, xa_s, xa_g, xa_sg, yb, yb_s, yb_g, yb_sg, keep0, solution_rows, keep_a, keep_b, hit, work, invb,
+    xa, xa_s, xa_g, xa_sg, yb, yb_s, yb_g, yb_sg, keep0, solution_rows, keep_a, keep_b, hit, work, invb, inv1, cross,
     pan, acc, sums, core_got, keep1, z_code, z_scale, z_got, z_sgot,
     load, send, recv,
 ):
@@ -153,41 +145,54 @@
     loads = {o: pltpu.make_async_copy(border.at[pl.ds((grp ^ o) * own, own)], big.at[o], load.at[o]) for o in range(groups)}
     loads["prior"] = pltpu.make_async_copy(prior_hbm, prior, load.at[groups])
     loads["inverse"] = pltpu.make_async_copy(inverse, minv, load.at[groups + 1])
-    for name in ["prior"] + list(range(groups)) + ["inverse"]:
+    loads["sel"] = pltpu.make_async_copy(sel_hbm, sel, load.at[groups + 2])
+    loads["asg"] = pltpu.make_async_copy(asg_hbm, asg, load.at[groups + 3])
+    loads["prob"] = pltpu.make_async_copy(prob_hbm, prob, load.at[groups + 4])
+    for name in ["sel"] + list(range(groups)) + ["prior", "inverse", "asg", "prob"]:
         loads[name].start()
     barrier = pltpu.get_barrier_semaphore()
     partners = [cpart] + list(chip.values()) + list(peer.values())
     for where in partners:
         pl.semaphore_signal(barrier, inc=1, device_id=where, device_id_type=MESH)
 
+    loads["sel"].wait()
     want = jnp.transpose(jnp.broadcast_to(sel[...], (LANES, width)))[:, :1]
     want = jnp.broadcast_to(want, (width, own))
     lanes = lax.broadcasted_iota(jnp.int32, (width, own), 1)
     first = (dev * groups + grp) * own
+    high = flat.shape[0]
+    half, quarter, bit = high // CORES, high // (CORES * XHI), high // count
+    at1 = core * half
+    part = size // CORES
+
+    def pick(which):
+        total = None
+        at = pl.multiple_of(which * part, LANES)
+        for o in range(groups):
+            if which is not core:
+                loads[o].wait()
+                base = (dev * groups + (grp ^ o)) * own
+                hot[o] = (want - base == lanes).astype(F32).astype(BF16)
+            got = dot(hot[o], big[o, :, pl.ds(at, part)], 1, 0)
+            total = got if total is None else total + got
+        total = total.astype(BF16)
+        for c in range(part // LANES):
+            flat[pl.ds(which * half + c * width, width), :] = total[:, c * LANES : (c + 1) * LANES]
+
+    pick(1 - core)
+    pl.semaphore_wait(barrier, len(partners))
+    fenced(lambda: mail.start("r1", lambda: flat.at[pl.ds((1 - core) * half, half)], got1, cpart))
+    pick(core)
     loads["prior"].wait()
     mine = dot((want - first == lanes).astype(F32).astype(BF16), prior[...], 1, 0).astype(BF16)
     for c in range(2):
         q0[pl.ds(c * width, width), :] = mine[:, c * LANES : (c + 1) * LANES]
-    total = None
-    for o in range(groups):
-        loads[o].wait()
-        base = (dev * groups + (grp ^ o)) * own
-        part = dot((want - base == lanes).astype(F32).astype(BF16), big[o], 1, 0)
-        total = part if total is None else total + part
-    total = total.astype(BF16)
-    for c in range(size // LANES):
-        flat[pl.ds(c * width, width), :] = total[:, c * LANES : (c + 1) * LANES]
-    pl.semaphore_wait(barrier, len(partners))
-
-    high = flat.shape[0]
-    half, quarter, bit = high // CORES, high // (CORES * XHI), high // count
+
     qhalf, qquart, qbit = 2 * width // CORES, 2 * width // (CORES * XHI), 2 * width // count
-    at1 = core * half
     at3 = at1 + xhi * quarter + z * bit
     qat1 = core * qhalf
     qat2 = qat1 + xhi * qquart
     qat3 = qat2 + z * qbit
-    mail.start("r1", flat.at[pl.ds((1 - core) * half, half)], got1, cpart)
     mail.start("q1", q0.at[pl.ds((1 - core) * qhalf, qhalf)], qh, cpart)
     mail.take("r1", got1, cpart)
     flat[pl.ds(at1, half), :] = flat[pl.ds(at1, half), :] + got1[...]
@@ -248,6 +253,8 @@
         picked[:, c * LANES : (c + 1) * LANES] = rows[pl.ds(c * width, width), :]
     loads["inverse"].wait()
     project[...] = dot(minv[...], picked[...], 1, 1).astype(BF16)
+    loads["asg"].wait()
+    loads["prob"].wait()
     scenario = asg[grp]
     weight = 0.0
     for i in range(groups):
@@ -259,7 +266,7 @@
     corner[...] = weight * dot(picked[cmine, :], project[...], 1, 0)
     for n, o in enumerate(near):
         mail.start("c1", corner, corner_got.at[n], peer[o], corner_got)
-    ra, rb = split(own, 0.56)
+    ra, rb = split(own, 0.53)
 
     def block(o):
         return weight * jnp.dot(big[o], project[...], preferred_element_type=F32)
@@ -285,6 +292,8 @@
     lots = q.at[pl.ds(0, XHI * (depth - 1) * qbit)]
     rest = corner_sum.at[pl.ds(0, (turn - 1) * cpiece)]
 
+    chalves = lambda: corner_sum.at[pl.ds(0, chalf)]
+
     def blocks(y):
         make(y)
         ship(y)
@@ -298,6 +307,7 @@
         here = corner_sum.at[cmine]
         for o in steps:
             mail.start("c2", here, here, zparts[o], lambda: rest)
+        mail.start("c3", here, here, cpart, chalves)
 
     def prior_out():
         mail.take("q5", q.at[pl.ds(qat1 + (1 - xhi) * qquart + z * qbit, qbit)], xpart)
@@ -328,8 +338,9 @@
     less = dot(picks, picks, 1, 1)
     if zparts:
         mail.take("c2", rest, xpart)
-    here = corner_sum.at[pl.ds(core * chalf, chalf)]
-    mail.start("c3", here, here, cpart)
+    for o in range(1, turn):
+        here = corner_sum.at[pl.ds(core * chalf + (z + o) % turn * cpiece, cpiece)]
+        mail.start("c3", here, here, cpart, chalves)
     mail.take("c3", corner_sum.at[pl.ds((1 - core) * chalf, chalf)], cpart)
     a = corner_sum[...] - less
     a = 0.5 * (a + jnp.transpose(a))
@@ -365,22 +376,28 @@
             mail.take(("yb", y), yb_g.at[y], peer[2 * y])
             lower = lower + decode(yb_g[y], yb_sg[y])
         keep0[ra:, :] = lower
+        whole = jnp.where(hit[...] > 0.5, 0.0, keep0[...])
+        left = dot(whole[:, :BASE], inv1[...], 1, 1, HIGHEST)
+        solution_rows[:, :BASE] = left
+        pan[0, :, :BASE] = left.astype(BF16)
+        keep0[:, BASE:] = whole[:, BASE:] - dot(left, cross[...], 1, 1, HIGHEST)
 
     hooks = [lambda: None for _ in range(width // PANEL)]
     for y, n in zip(ys, (0, 1, 4)):
         hooks[n] = functools.partial(fenced, onward, y)
     hooks[7] = functools.partial(fenced, across)
     hooks[15] = functools.partial(fenced, gather)
-    w = inverse_factor(a, work, invb, hooks)
+    inv1[...] = eliminated(a[:BASE, :BASE], work, invb, hooks)
+    cross[...] = dot(a[BASE:, :BASE], inv1[...], 1, 1, HIGHEST)
+    inv2 = eliminated(a[BASE:, BASE:] - dot(cross[...], cross[...], 1, 1, HIGHEST), work, invb, hooks)
 
     pa, pb = split(own, 0.53)
     top, low = pl.ds(0, pa), pl.ds(pa, pb)
 
     def solve(rows):
-        solved = dot(keep0[rows, :], w, 1, 1, HIGHEST)
-        solved = jnp.where(hit[rows, :] > 0.5, 0.0, solved)
-        solution_rows[rows, :] = solved
-        pan[0, rows, :] = solved.astype(BF16)
+        right = dot(keep0[rows, BASE:], inv2, 1, 1, HIGHEST)
+        solution_rows[rows, BASE:] = right
+        pan[0, rows, BASE:] = right.astype(BF16)
 
     tops = [pl.ds(0, pa // 32 * 16), pl.ds(pa // 32 * 16, pa - pa // 32 * 16)]
     lows = [pl.ds(pa, pb // 32 * 16), pl.ds(pa + pb // 32 * 16, pb - pb // 32 * 16)]
@@ -471,9 +488,12 @@
     value = keep1[z, xhi]
     for n in range(len(chips)):
         value = value + decode(z_got[n], z_sgot[n])
-    out[...] = value
+    last[...] = value
+    finished = pltpu.make_async_copy(last, out, load.at[groups + 1])
+    finished.start()
     written.wait()
     mail.close()
+    finished.wait()
     assert len(mail.ids) <= send.shape[0], len(mail.ids)
 
 
@@ -487,22 +507,25 @@
     piece = size // count
     high = size // LANES * width
     ny = groups // XLO
-    ra, rb = split(own, 0.56)
+    ra, rb = split(own, 0.53)
     dma, vmem = pltpu.SemaphoreType.DMA, pltpu.VMEM
-    vm = pl.BlockSpec(memory_space=vmem)
     anyspace = pl.BlockSpec(memory_space=pl.ANY)
-    sm = pl.BlockSpec(memory_space=pltpu.SMEM)
     return pl.pallas_call(
         functools.partial(kernel, groups, count),
         out_shape=(jax.ShapeDtypeStruct((own, width), F32), jax.ShapeDtypeStruct((piece, width), F32)),
-        in_specs=[anyspace, anyspace, anyspace, vm, sm, sm],
-        out_specs=(anyspace, vm),
+        in_specs=[anyspace] * 6,
+        out_specs=(anyspace, anyspace),
         scratch_shapes=[
+            vmem((1, width), jnp.int32),
+            pltpu.SMEM((groups,), jnp.int32),
+            pltpu.SMEM((groups,), F32),
+            vmem((piece, width), F32),
             vmem((groups, own, size), BF16),
             vmem((size, size), BF16),
             vmem((own, width), BF16),
             vmem((high, LANES), BF16),
             vmem((high, LANES), BF16),
+            vmem((groups, width, own), BF16),
             vmem((high // CORES, LANES), BF16),
             vmem((others, high // count, LANES), BF16),
             vmem((2 * width, LANES), BF16),
@@ -540,6 +563,8 @@
             vmem((own, width), F32),
             vmem((BASE, 2 * BASE), F32),
             vmem((BASE, BASE), F32),
+            vmem((BASE, BASE), F32),
+            vmem((BASE, BASE), F32),
             vmem((groups, own, width), BF16),
             vmem((width, size), F32),
             vmem((CORES, depth, XHI, piece, width), F32),
@@ -549,7 +574,7 @@
             vmem((1, width), F32),
             vmem((others, piece, width), I16),
             vmem((others, 1, width), F32),
-            dma((groups + 2,)),
+            dma((groups + 5,)),
             dma((messages,)),
             dma((messages,)),
         ],
@@ -560,18 +585,35 @@
     )(border, inverse, prior, sel, asg, prob)
 
 
-def finish_kernel(panel, residual, panel_out, residual_out):
-    panel_out[...] = panel[...]
-    residual_out[...] = residual[...]
+def finish_kernel(panel, residual, panel_out, residual_out, held, kept, came, went):
+    rows = panel.shape[0] // 4
+    parts = [(panel.at[pl.ds(n * rows, rows)], held.at[n], panel_out.at[pl.ds(n * rows, rows)]) for n in range(4)]
+    parts = [(residual, kept, residual_out)] + parts
+    ins = [pltpu.make_async_copy(src, mid, came.at[n]) for n, (src, mid, _) in enumerate(parts)]
+    outs = [pltpu.make_async_copy(mid, dst, went.at[n]) for n, (_, mid, dst) in enumerate(parts)]
+    for go in ins:
+        go.start()
+    for go, out in zip(ins, outs):
+        go.wait()
+        out.start()
+    for out in outs:
+        out.wait()
 
 
 def finish(panel, residual):
-    vm = pl.BlockSpec(memory_space=pltpu.VMEM)
+    anyspace = pl.BlockSpec(memory_space=pl.ANY)
+    rows, width = panel.shape
     return pl.pallas_call(
         finish_kernel,
         out_shape=(jax.ShapeDtypeStruct(panel.shape, F32), jax.ShapeDtypeStruct(residual.shape, F32)),
-        in_specs=[vm, vm],
-        out_specs=(vm, vm),
+        in_specs=[anyspace, anyspace],
+        out_specs=(anyspace, anyspace),
+        scratch_shapes=[
+            pltpu.VMEM((4, rows // 4, width), F32),
+            pltpu.VMEM(residual.shape, F32),
+            pltpu.SemaphoreType.DMA((5,)),
+            pltpu.SemaphoreType.DMA((5,)),
+        ],
         name="finish",
     )(panel, residual)
 

time: 90.2 us -> 88 us (0.976)
  Pallas kernels: 89.4 us -> 87 us
    pallas_call x1, Pallas kernels: 87.6 us -> 85.2 us  [call(): pl.pallas_call(functools.partial(kernel, groups, count), out_shape=(jax.S...]
where the time goes in v5:
time: 88 us; the launch traced here: 87.8 us
  Pallas kernels  87 us (99%)
    pallas_call x1, Pallas kernels, call(): pl.pallas_call(functools.partial(kernel, groups, count), out_shape=(jax.S...  85.2 us
    pallas_call x1, Pallas kernels, finish(): pl.pallas_call(finish_kernel, out_shape=(jax.ShapeDtypeStruct(panel.shape...  1.86 us

profile of v5, /device:TPU:1, one launch (start us, length us, event | category | flops | bytes accessed | tf_op | source)
XLA Modules:
  0.0 87.8 jit_solution(9295638669114653725)
XLA Ops:
  0.6 85.2 %panel.1 = (f32[512,256]{1,0:T(8,128)}, f32[32,256]{1,0:T(8,128)}) custom-call(bf16[4096,1024]{1,0:T(8,128)(2,1)} %bitcast.4, bf16[1024,1024]{1,0:T(8,128)(2,1)} %bitcast.5, bf16[512,256]{1,0:T(8,128)(2,1)} %prior_hbm.1, s32[1,256]{1,0:T(1,128)} %bitcast.6, s32[8]{0:T(128)} %asg_hbm.1, f32[8]{0:T(128)} %prob_hbm.1), custom_call_target="tpu_custom_call" | custom-call | tf_op jit(solution)/shard_map/panel/pallas_call | solution.py:513
  85.8 1.9 %finish.1 = (f32[512,256]{1,0:T(8,128)}, f32[32,256]{1,0:T(8,128)}) custom-call(f32[512,256]{1,0:T(8,128)} %get-tuple-element.6.panel, f32[32,256]{1,0:T(8,128)} %get-tuple-element.7.residual), custom_call_target="tpu_custom_call" | custom-call | tf_op jit(solution)/shard_map/finish/pallas_call | solution.py:606

commit v6 on v5

--- a/solution.py
+++ b/solution.py
@@ -90,28 +90,43 @@
 
 
 class Mail:
-    def __init__(self, send, recv):
-        self.send, self.recv, self.ids, self.started = send, recv, {}, {}
-
-    def copy(self, key, src, dst, where):
+    LOT = 3072 * 2 * LANES
+
+    def __init__(self, send, recv, spare, spare_scales):
+        self.send, self.recv, self.spare, self.spare_scales = send, recv, spare, spare_scales
+        self.ids, self.lots, self.scales = {}, [0], 0
+
+    def copy(self, key, src, dst, where, lot=0):
         k = self.ids.setdefault(key, len(self.ids))
         return pltpu.make_async_remote_copy(
-            src_ref=src, dst_ref=dst, send_sem=self.send.at[k], recv_sem=self.recv.at[k],
+            src_ref=src, dst_ref=dst, send_sem=self.send.at[lot], recv_sem=self.recv.at[k],
             device_id=where, device_id_type=MESH,
         )
 
-    def start(self, key, src, dst, where, whole=None):
-        self.copy(key, src() if callable(src) else src, dst, where).start()
-        assert whole is not None or key not in self.started, key
-        self.started[key] = (src if whole is None else whole, where)
+    def start(self, key, src, dst, where):
+        shape = src.shape
+        if src.dtype == F32 and shape[-2] == 1:
+            self.scales += math.prod(shape[:-2])
+            lot = 0
+        else:
+            size = math.prod(shape) * jnp.dtype(src.dtype).itemsize
+            if self.lots[-1] + size > self.LOT:
+                self.lots.append(0)
+            self.lots[-1] += size
+            lot = len(self.lots)
+        self.copy(key, src, dst, where, lot).start()
 
     def take(self, key, dst, where):
         self.copy(key, dst, dst, where).wait_recv()
 
-    def close(self):
-        for key, (ref, where) in self.started.items():
-            ref = ref() if callable(ref) else ref
-            self.copy(key, ref, ref, where).wait_send()
+    def close(self, where):
+        if self.scales:
+            ref = self.spare_scales.at[pl.ds(0, self.scales)]
+            self.copy("r1", ref, ref, where).wait_send()
+        for n, size in enumerate(self.lots):
+            ref = self.spare.at[pl.ds(0, size // (2 * LANES))]
+            self.copy("r1", ref, ref, where, n + 1).wait_send()
+        assert len(self.ids) <= self.recv.shape[0] and len(self.lots) < self.send.shape[0]
 
 
 def kernel(
@@ -120,7 +135,7 @@
     corner, corner_got, corner_sum, ya, ya_s, ya_g, ya_sg, xb, xb_s, xb_g, xb_sg,
     xa, xa_s, xa_g, xa_sg, yb, yb_s, yb_g, yb_sg, keep0, solution_rows, keep_a, keep_b, hit, work, invb, inv1, cross,
     pan, acc, sums, core_got, keep1, z_code, z_scale, z_got, z_sgot,
-    load, send, recv,
+    spare, spare_scales, load, send, recv,
 ):
     grp, dev = lax.axis_index("grp"), lax.axis_index("dev")
     depth = count // (CORES * XHI)
@@ -137,7 +152,7 @@
     peer = {o: (grp ^ o, dev) for o in near}
     width, size = picked.shape
     own = prior.shape[0]
-    mail = Mail(send, recv)
+    mail = Mail(send, recv, spare, spare_scales)
 
     def fenced(f, *args):
         pl.when(grp >= 0)(functools.partial(f, *args))
@@ -181,7 +196,7 @@
 
     pick(1 - core)
     pl.semaphore_wait(barrier, len(partners))
-    fenced(lambda: mail.start("r1", lambda: flat.at[pl.ds((1 - core) * half, half)], got1, cpart))
+    fenced(lambda: mail.start("r1", flat.at[pl.ds((1 - core) * half, half)], got1, cpart))
     pick(core)
     loads["prior"].wait()
     mine = dot((want - first == lanes).astype(F32).astype(BF16), prior[...], 1, 0).astype(BF16)
@@ -198,7 +213,7 @@
     flat[pl.ds(at1, half), :] = flat[pl.ds(at1, half), :] + got1[...]
     for c in chips:
         there = at1 + (xhi ^ c[1]) * quarter + ((z + c[0]) % depth) * bit
-        mail.start("r2", flat.at[pl.ds(there, bit)], got2.at[slot[c]], chip[c], got2)
+        mail.start("r2", flat.at[pl.ds(there, bit)], got2.at[slot[c]], chip[c])
     mail.take("q1", qh, cpart)
     q0[pl.ds(qat1, qhalf), :] = q0[pl.ds(qat1, qhalf), :] + qh[...]
     mail.start("q2", q0.at[pl.ds(qat1 + (1 - xhi) * qquart, qquart)], qx, xpart)
@@ -208,7 +223,7 @@
     mail.take("q2", qx, xpart)
     q0[pl.ds(qat2, qquart), :] = q0[pl.ds(qat2, qquart), :] + qx[...]
     for o in zparts:
-        mail.start("q3", q0.at[pl.ds(qat2 + ((z + o) % depth) * qbit, qbit)], qz.at[o - 1], zparts[o], qz)
+        mail.start("q3", q0.at[pl.ds(qat2 + ((z + o) % depth) * qbit, qbit)], qz.at[o - 1], zparts[o])
     mail.take("r2", got2, xpart)
     value = flat[pl.ds(at3, bit), :]
     for c in chips:
@@ -218,9 +233,9 @@
     rings = [chips[i : i + 5] for i in range(0, len(chips), 5)]
     for n, ring in enumerate(rings):
         for c in ring:
-            mail.start(("r3", n), here, here, chip[c], got2.at[pl.ds(0, len(ring))])
+            mail.start(("r3", n), here, here, chip[c])
     other = rows.at[pl.ds((1 - core) * half, half)]
-    mail.start("r4", here, here, cpart, other)
+    mail.start("r4", here, here, cpart)
     value = q0[pl.ds(qat3, qbit), :]
     if zparts:
         mail.take("q3", qz, xpart)
@@ -228,13 +243,13 @@
         value = value + qz[o - 1]
     qv[...] = value
     for n, o in enumerate(near):
-        mail.start("q4", qv, qg.at[n], peer[o], qg)
+        mail.start("q4", qv, qg.at[n], peer[o])
 
     def forward(n):
         mail.take(("r3", n), got2.at[pl.ds(0, len(rings[n]))], xpart)
         for c in rings[n]:
             there = rows.at[pl.ds(at1 + (xhi ^ c[1]) * quarter + ((z + depth - c[0]) % depth) * bit, bit)]
-            mail.start("r4", there, there, cpart, other)
+            mail.start("r4", there, there, cpart)
 
     order = list(range(len(rings)))[::-1]
     forward(order[0])
@@ -265,7 +280,7 @@
     cmine = pl.ds(core * chalf + z % turn * cpiece, cpiece)
     corner[...] = weight * dot(picked[cmine, :], project[...], 1, 0)
     for n, o in enumerate(near):
-        mail.start("c1", corner, corner_got.at[n], peer[o], corner_got)
+        mail.start("c1", corner, corner_got.at[n], peer[o])
     ra, rb = split(own, 0.53)
 
     def block(o):
@@ -283,16 +298,14 @@
             keep_a[...] = side[:ra]
 
     def ship(y):
-        mail.start(("xbs", y), lambda: xb_s.at[y], xb_sg.at[y], peer[1])
-        mail.start(("xb", y), lambda: xb.at[y], xb_g.at[y], peer[1])
+        mail.start(("xbs", y), xb_s.at[y], xb_sg.at[y], peer[1])
+        mail.start(("xb", y), xb.at[y], xb_g.at[y], peer[1])
         if y:
-            mail.start(("yas", y), lambda: ya_s.at[y], ya_sg.at[y], peer[2 * y])
-            mail.start(("ya", y), lambda: ya.at[y], ya_g.at[y], peer[2 * y])
+            mail.start(("yas", y), ya_s.at[y], ya_sg.at[y], peer[2 * y])
+            mail.start(("ya", y), ya.at[y], ya_g.at[y], peer[2 * y])
 
     lots = q.at[pl.ds(0, XHI * (depth - 1) * qbit)]
     rest = corner_sum.at[pl.ds(0, (turn - 1) * cpiece)]
-
-    chalves = lambda: corner_sum.at[pl.ds(0, chalf)]
 
     def blocks(y):
         make(y)
@@ -306,21 +319,21 @@
         corner_sum[cmine, :] = value
         here = corner_sum.at[cmine]
         for o in steps:
-            mail.start("c2", here, here, zparts[o], lambda: rest)
-        mail.start("c3", here, here, cpart, chalves)
+            mail.start("c2", here, here, zparts[o])
+        mail.start("c3", here, here, cpart)
 
     def prior_out():
         mail.take("q5", q.at[pl.ds(qat1 + (1 - xhi) * qquart + z * qbit, qbit)], xpart)
         for o in zparts:
             for x in range(XHI):
                 here = q.at[pl.ds(qat1 + x * qquart + z * qbit, qbit)]
-                mail.start("q6", here, here, zparts[o], lambda: lots)
+                mail.start("q6", here, here, zparts[o])
 
     def prior_over():
         if zparts:
             mail.take("q6", lots, xpart)
-        here = lambda: q.at[pl.ds(qat1, qhalf)]
-        mail.start("q7", here, here(), cpart)
+        here = q.at[pl.ds(qat1, qhalf)]
+        mail.start("q7", here, here, cpart)
 
     for y in ys[:1]:
         fenced(blocks, y)
@@ -340,7 +353,7 @@
         mail.take("c2", rest, xpart)
     for o in range(1, turn):
         here = corner_sum.at[pl.ds(core * chalf + (z + o) % turn * cpiece, cpiece)]
-        mail.start("c3", here, here, cpart, chalves)
+        mail.start("c3", here, here, cpart)
     mail.take("c3", corner_sum.at[pl.ds((1 - core) * chalf, chalf)], cpart)
     a = corner_sum[...] - less
     a = 0.5 * (a + jnp.transpose(a))
@@ -349,8 +362,8 @@
         mail.take(("xbs", y), xb_sg.at[y], peer[1])
         mail.take(("xb", y), xb_g.at[y], peer[1])
         encode(keep_b[y] + decode(xb_g[y], xb_sg[y]), yb.at[y], yb_s.at[y])
-        mail.start(("ybs", y), lambda: yb_s.at[y], yb_sg.at[y], peer[2 * y])
-        mail.start(("yb", y), lambda: yb.at[y], yb_g.at[y], peer[2 * y])
+        mail.start(("ybs", y), yb_s.at[y], yb_sg.at[y], peer[2 * y])
+        mail.start(("yb", y), yb.at[y], yb_g.at[y], peer[2 * y])
 
     def across():
         value, here = keep_a[...], keep0[:ra, :]
@@ -481,8 +494,8 @@
     z_scale[...] = peak * (1.0 / TOP)
     z_code[...] = jnp.round(value * (TOP / peak)).astype(jnp.int32).astype(I16).reshape(z_code.shape)
     for c in chips:
-        mail.start("s2s", z_scale, z_sgot.at[slot[c]], chip[c], z_sgot)
-        mail.start("s2", z_code.at[(z + c[0]) % depth, xhi ^ c[1]], z_got.at[slot[c]], chip[c], z_got)
+        mail.start("s2s", z_scale, z_sgot.at[slot[c]], chip[c])
+        mail.start("s2", z_code.at[(z + c[0]) % depth, xhi ^ c[1]], z_got.at[slot[c]], chip[c])
     mail.take("s2s", z_sgot, xpart)
     mail.take("s2", z_got, xpart)
     value = keep1[z, xhi]
@@ -492,9 +505,8 @@
     finished = pltpu.make_async_copy(last, out, load.at[groups + 1])
     finished.start()
     written.wait()
-    mail.close()
+    mail.close(cpart)
     finished.wait()
-    assert len(mail.ids) <= send.shape[0], len(mail.ids)
 
 
 def call(groups, count, border, inverse, prior, sel, asg, prob):
@@ -574,8 +586,10 @@
             vmem((1, width), F32),
             vmem((others, piece, width), I16),
             vmem((others, 1, width), F32),
+            vmem((3072, LANES), BF16),
+            vmem((64, 1, width), F32),
             dma((groups + 5,)),
-            dma((messages,)),
+            dma((12,)),
             dma((messages,)),
         ],
         compiler_params=pltpu.CompilerParams(

time: 88 us -> 87.5 us (level)
  no operation moved by 1% of the time
where the time goes in v6:
time: 87.5 us; the launch traced here: 87.4 us
  Pallas kernels  86.6 us (99%)
    pallas_call x1, Pallas kernels, call(): pl.pallas_call(functools.partial(kernel, groups, count), out_shape=(jax.S...  84.8 us
    pallas_call x1, Pallas kernels, finish(): pl.pallas_call(finish_kernel, out_shape=(jax.ShapeDtypeStruct(panel.shape...  1.86 us

profile of v6, /device:TPU:1, one launch (start us, length us, event | category | flops | bytes accessed | tf_op | source)
XLA Modules:
  0.0 87.4 jit_solution(17680644033173293688)
XLA Ops:
  0.6 84.8 %panel.1 = (f32[512,256]{1,0:T(8,128)}, f32[32,256]{1,0:T(8,128)}) custom-call(bf16[4096,1024]{1,0:T(8,128)(2,1)} %bitcast.4, bf16[1024,1024]{1,0:T(8,128)(2,1)} %bitcast.5, bf16[512,256]{1,0:T(8,128)(2,1)} %prior_hbm.1, s32[1,256]{1,0:T(1,128)} %bitcast.6, s32[8]{0:T(128)} %asg_hbm.1, f32[8]{0:T(128)} %prob_hbm.1), custom_call_target="tpu_custom_call" | custom-call | tf_op jit(solution)/shard_map/panel/pallas_call | solution.py:525
  85.4 1.9 %finish.1 = (f32[512,256]{1,0:T(8,128)}, f32[32,256]{1,0:T(8,128)}) custom-call(f32[512,256]{1,0:T(8,128)} %get-tuple-element.6.panel, f32[32,256]{1,0:T(8,128)} %get-tuple-element.7.residual), custom_call_target="tpu_custom_call" | custom-call | tf_op jit(solution)/shard_map/finish/pallas_call | solution.py:620

commit v7 on v6

--- a/solution.py
+++ b/solution.py
@@ -494,8 +494,9 @@
     z_scale[...] = peak * (1.0 / TOP)
     z_code[...] = jnp.round(value * (TOP / peak)).astype(jnp.int32).astype(I16).reshape(z_code.shape)
     for c in chips:
+        mail.start("s2", z_code.at[(z + c[0]) % depth, xhi ^ c[1]], z_got.at[slot[c]], chip[c])
+    for c in chips:
         mail.start("s2s", z_scale, z_sgot.at[slot[c]], chip[c])
-        mail.start("s2", z_code.at[(z + c[0]) % depth, xhi ^ c[1]], z_got.at[slot[c]], chip[c])
     mail.take("s2s", z_sgot, xpart)
     mail.take("s2", z_got, xpart)
     value = keep1[z, xhi]

time: 87.5 us -> 88.7 us (1.014)
  Pallas kernels: 86.6 us -> 87.8 us
    pallas_call x1, Pallas kernels: 84.8 us -> 86 us  [call(): pl.pallas_call(functools.partial(kernel, groups, count), out_shape=(jax.S...]
where the time goes in v7:
time: 88.7 us; the launch traced here: 88.6 us
  Pallas kernels  87.8 us (99%)
    pallas_call x1, Pallas kernels, call(): pl.pallas_call(functools.partial(kernel, groups, count), out_shape=(jax.S...  86 us
    pallas_call x1, Pallas kernels, finish(): pl.pallas_call(finish_kernel, out_shape=(jax.ShapeDtypeStruct(panel.shape...  1.86 us

profile of v7, /device:TPU:1, one launch (start us, length us, event | category | flops | bytes accessed | tf_op | source)
XLA Modules:
  0.0 88.6 jit_solution(15566819654378048551)
XLA Ops:
  0.6 86.0 %panel.1 = (f32[512,256]{1,0:T(8,128)}, f32[32,256]{1,0:T(8,128)}) custom-call(bf16[4096,1024]{1,0:T(8,128)(2,1)} %bitcast.4, bf16[1024,1024]{1,0:T(8,128)(2,1)} %bitcast.5, bf16[512,256]{1,0:T(8,128)(2,1)} %prior_hbm.1, s32[1,256]{1,0:T(1,128)} %bitcast.6, s32[8]{0:T(128)} %asg_hbm.1, f32[8]{0:T(128)} %prob_hbm.1), custom_call_target="tpu_custom_call" | custom-call | tf_op jit(solution)/shard_map/panel/pallas_call | solution.py:526
  86.6 1.9 %finish.1 = (f32[512,256]{1,0:T(8,128)}, f32[32,256]{1,0:T(8,128)}) custom-call(f32[512,256]{1,0:T(8,128)} %get-tuple-element.6.panel, f32[32,256]{1,0:T(8,128)} %get-tuple-element.7.residual), custom_call_target="tpu_custom_call" | custom-call | tf_op jit(solution)/shard_map/finish/pallas_call | solution.py:621
